TPU v7x, 32 devices: a whole 2x2x4 slice. The times are simulated.
32 devices in a mesh: ab: 2 (over y), cd: 16 (over z, x, core).
Axes of the slice: x: 2, y: 2, z: 4, core: 2. Of those that a mesh axis runs over, the one named last changes fastest.
Arguments:
- amplitudes: float32 [768, 16384], P('cd', 'ab'), may hold values from -1.25 to 1.25
- driver: float32 [768, 16384], P('cd', 'ab'), may hold values from -6 to 6
- ladder: bfloat16 [16384, 16384], P('ab', 'cd'), may hold values from -0.125 to 0.125
- block_mask: int32 [128, 128], P('ab', 'cd'), may hold values 0 or 1
- pair_list: int32 [768], replicated, may hold values from 0 to 1023, as said below
- occ_energy: float32 [32], replicated, may hold values from -2 to -0.5
- virt_energy: float32 [128], replicated, may hold values from 0.5 to 3
Outputs:
- new_amplitudes: float32 [768, 16384], P('cd', 'ab')
Inputs may be any that keep to these rules, and one draw needn't show every extreme that they name: `pair_list`: the entries are distinct occupied pairs i * 32 + j. Rows come in aligned blocks of two: a pair with i != j shares its block with the pair (j, i); pairs with i == j stand two to a block. Pairs 0 and 1023 are always listed.
All inputs are finite; a program needn't handle non-finite values. No bound on the sum of `block_mask` on one device may be relied on, other than what follows from the above.
Results may differ from a plain program's by a relative error of at most 0.008.
Values may be sent and summed in bfloat16 or wider, within the bound.
A program may use at most 128 MiB of HBM per device.

v0:
```python
import jax
import jax.numpy as jnp
from jax import lax
from jax.sharding import PartitionSpec as P

NV = 128
NOCC = 32
BLK = 128
ITERS = 2


def flip_tiles(tiles, tile_width):
    row_count, tile_count = tiles.shape[:2]
    turned = jnp.swapaxes(tiles.reshape(row_count, tile_count, tile_width, tile_width), 2, 3)
    return turned.reshape(row_count, tile_count * tile_width * tile_width)


def body(amplitudes, driver, ladder, block_mask, pair_list, occ_energy, virt_energy):
    ab_count = lax.axis_size("ab")
    ab_index = lax.axis_index("ab")
    cd_index = lax.axis_index("cd")
    rows_dev, cols_dev = amplitudes.shape
    out_rows, in_cols = ladder.shape
    tile_width = NV // ab_count
    tile_area = tile_width * tile_width
    weights = ladder.reshape(out_rows // BLK, BLK, in_cols // BLK, BLK)
    weights = (weights * block_mask.astype(jnp.bfloat16)[:, None, :, None]).reshape(
        out_rows, in_cols
    )
    pairs_local = ab_index * cols_dev + jnp.arange(cols_dev, dtype=jnp.int32)
    big_a = pairs_local // (tile_width * NV)
    big_b = pairs_local // tile_area % ab_count
    first = big_a * tile_width + pairs_local // tile_width % tile_width
    second = big_b * tile_width + pairs_local % tile_width
    virt_index = jnp.arange(NV, dtype=jnp.int32)
    picks = (first[:, None] == virt_index).astype(jnp.float32) + (
        second[:, None] == virt_index
    ).astype(jnp.float32)
    col_energy = jnp.dot(picks, virt_energy, precision=lax.Precision.HIGHEST)
    row_pairs = lax.dynamic_slice_in_dim(pair_list, cd_index * rows_dev, rows_dev)
    occ_index = jnp.arange(NOCC, dtype=jnp.int32)
    occ_picks = (row_pairs[:, None] // NOCC == occ_index).astype(jnp.float32)
    occ_picks = occ_picks + (row_pairs[:, None] % NOCC == occ_index).astype(jnp.float32)
    row_energy = jnp.dot(occ_picks, occ_energy, precision=lax.Precision.HIGHEST)
    denominator = col_energy[None, :] - row_energy[:, None]
    local_diagonal = row_pairs // NOCC == row_pairs % NOCC
    row_index = jnp.arange(rows_dev, dtype=jnp.int32)
    mirror_row = jnp.where(local_diagonal, row_index, row_index ^ 1)
    row_swap = (mirror_row[:, None] == row_index).astype(jnp.bfloat16)
    state = amplitudes
    for step in range(ITERS):
        rounded = state.astype(jnp.bfloat16)
        regrouped = lax.all_to_all(rounded, "cd", split_axis=1, concat_axis=0, tiled=True)
        partial_value = lax.dot_general(
            lax.all_gather(regrouped, "ab", axis=1, tiled=True),
            weights,
            (((1,), (1,)), ((), ())),
            preferred_element_type=jnp.float32,
        )
        received = lax.psum_scatter(
            partial_value.astype(jnp.bfloat16), "cd", scatter_dimension=0, tiled=True
        )
        swapped = jnp.dot(row_swap, received, preferred_element_type=jnp.float32)
        tiles = lax.all_to_all(
            swapped.astype(jnp.bfloat16).reshape(rows_dev, ab_count, tile_area),
            "ab",
            split_axis=1,
            concat_axis=1,
            tiled=True,
        )
        symmetric = received.astype(jnp.float32) + flip_tiles(tiles, tile_width).astype(jnp.float32)
        state = (driver + symmetric) / denominator
    return state


def solution(mesh):
    placed = (P("cd", "ab"), P("cd", "ab"), P("ab", "cd"), P("ab", "cd"), P(), P(), P())
    return jax.shard_map(body, mesh=mesh, in_specs=placed, out_specs=P("cd", "ab"), check_vma=False)
```

profile of v0, /device:TPU:0, one launch (start us, length us, event | category | flops | bytes accessed | tf_op | source)
XLA Modules:
  0.0 506.0 jit_solution(11198391696417357768)
XLA Ops:
  8.1 27.5 %all_to_all.48 = bf16[48,16,512]{2,0,1:T(8,128)(2,1)} all-to-all(bf16[48,16,512]{2,0,1:T(8,128)(2,1)S(1)} %bitcast.62), channel_id=1, replica_groups=mesh['ab'=2,'cd'=16] {'cd'}, dimensions={1} | all-to-all | bytes 1572864 | tf_op jit(solution)/shard_map/all_to_all | solution.py:53
  35.9 26.4 %all-gather.3.cloned.1.call-done = bf16[768,1024]{1,0:T(8,128)(2,1)} async-done(((bf16[768,512]{1,0:T(8,128)(2,1)}), bf16[768,1024]{1,0:T(8,128)(2,1)}) %all-gather.3.cloned.1.call-update) | async-done | bytes 1572880 | tf_op jit(solution)/shard_map/all_gather | solution.py:55
  62.3 6.1 %mul.31 = bf16[64,128,8,128]{3,2,1,0:T(8,128)(2,1)} broadcast(bf16[64,8]{1,0:T(8,128)(2,1)S(1)} %copy.52), dimensions={0,2} | broadcast | bytes 16778240 | tf_op jit(solution)/shard_map/mul | solution.py:27
  68.4 22.4 %fusion = bf16[768,8192]{0,1:T(8,128)(2,1)} fusion(bf16[768,1024]{1,0:T(8,128)(2,1)S(1)} %copy-done.3, bf16[8192,1024]{1,0:T(8,128)(2,1)} %param.9, bf16[1024,8,8,128]{3,2,1,0:T(8,128)(2,1)} %bitcast.55), kind=kOutput, calls=%fused_computation.3 | convolution fusion | flops 12899581952 | bytes 47710208 | tf_op jit(solution)/shard_map/dot_general | solution.py:54
  90.8 16.7 %copy.62 = bf16[768,8192]{1,0:T(8,128)(2,1)} copy(bf16[768,8192]{0,1:T(8,128)(2,1)} %fusion) | data formatting | bytes 25165824
  108.3 134.0 %reduce-scatter.7.cloned.1.call-done = bf16[48,8192]{1,0:T(8,128)(2,1)} async-done(((bf16[768,8192]{1,0:T(8,128)(2,1)}), bf16[48,8192]{1,0:T(8,128)(2,1)}) %reduce-scatter.7.cloned.1.call-update) | async-done | bytes 786448
  242.2 1.5 convolution_convert_fusion.3
  244.7 3.5 all-to-all-start.1
  248.6 6.4 %fusion.1 = f32[1,8192]{1,0:T(1,128)S(1)} fusion(s32[8192]{0:T(1024)S(1)} %get-tuple-element.9, s32[8192]{0:T(1024)S(1)} %get-tuple-element.8, f32[128]{0:T(128)S(1)} %copy-done), kind=kOutput, calls=%fused_computation.6 | convolution fusion | flops 17825792 | bytes 98816 | tf_op jit(solution)/shard_map/dot_general | solution.py:39
  255.0 3.5 all-to-all-done.1
  258.5 2.4 reshape.139
  260.9 2.4 copy.56
  263.3 1.9 reshape.137
  265.2 2.5 fusion.7
  267.7 25.0 %all_to_all.49 = bf16[48,16,512]{2,0,1:T(8,128)(2,1)} all-to-all(bf16[48,16,512]{2,0,1:T(8,128)(2,1)S(1)} %bitcast.63), channel_id=1, replica_groups=mesh['ab'=2,'cd'=16] {'cd'}, dimensions={1} | all-to-all | bytes 1572864 | tf_op jit(solution)/shard_map/all_to_all | solution.py:53
  293.0 25.4 %all-gather.5.cloned.1.call-done = bf16[768,1024]{1,0:T(8,128)(2,1)} async-done(((bf16[768,512]{1,0:T(8,128)(2,1)}), bf16[768,1024]{1,0:T(8,128)(2,1)}) %all-gather.5.cloned.1.call-update) | async-done | bytes 1572880 | tf_op jit(solution)/shard_map/all_gather | solution.py:55
  318.4 21.7 %convolution_convert_fusion = bf16[768,8192]{1,0:T(8,128)(2,1)} fusion(bf16[768,1024]{1,0:T(8,128)(2,1)} %all-gather.5.cloned.1.call-done, bf16[8192,1024]{1,0:T(8,128)(2,1)} %param.9, bf16[1024,8,8,128]{3,2,1,0:T(8,128)(2,1)} %bitcast.56), kind=kOutput, calls=%fused_computation.1 | convolution fusion | flops 12899581952 | bytes 47710208 | tf_op jit(solution)/shard_map/dot_general | solution.py:54
  340.1 134.8 %reduce-scatter.9.cloned.1.call-done = bf16[48,8192]{1,0:T(8,128)(2,1)} async-done(((bf16[768,8192]{1,0:T(8,128)(2,1)}), bf16[48,8192]{1,0:T(8,128)(2,1)}) %reduce-scatter.9.cloned.1.call-update) | async-done | bytes 786448
  474.9 1.5 convolution_convert_fusion.2
  476.5 12.7 %all_to_all.50 = bf16[48,2,4096]{2,0,1:T(8,128)(2,1)S(1)} all-to-all(bf16[48,2,4096]{2,0,1:T(8,128)(2,1)S(1)} %bitcast.65), channel_id=1, replica_groups=mesh['ab'=2,'cd'=16] {'ab'}, dimensions={1} | all-to-all | bytes 1572864 | tf_op jit(solution)/shard_map/all_to_all | solution.py:64
  489.2 2.4 reshape.140
  491.6 2.4 copy.61
  494.0 1.9 reshape.138
  495.9 3.6 subtract_divide_fusion
  (28 shorter events, 4.2 us)
Async XLA Ops:
  6.5 242.1 %copy-start = (f32[128]{0:T(128)S(1)}, f32[128]{0:T(128)}, u32[]{:S(2)}) copy-start(f32[128]{0:T(128)} %param.13) | copy-start | bytes 1540
  6.5 29.2 %copy-start.2 = (s32[64,8]{0,1:T(8,128)S(1)}, s32[64,8]{0,1:T(8,128)}, u32[]{:S(2)}) copy-start(s32[64,8]{0,1:T(8,128)} %param.10) | copy-start | bytes 6148
  6.5 55.8 %all-gather.3.cloned.1.call-start = ((), (), s32[]{:S(2)}) async-start(), calls=%async_computation.6 | async-start | bytes 2359296 | tf_op jit(solution)/shard_map/all_gather | solution.py:55
  35.7 206.5 %reduce-scatter.7.cloned.1.call-start = ((), (), s32[]{:S(2)}) async-start(), calls=%async_computation.8 | async-start | bytes 13369344
  62.3 6.1 %copy-start.3 = (bf16[768,1024]{1,0:T(8,128)(2,1)S(1)}, bf16[768,1024]{1,0:T(8,128)(2,1)}, u32[]{:S(2)}) copy-start(bf16[768,1024]{1,0:T(8,128)(2,1)} %all-gather.3.cloned.1.call-done) | copy-start | bytes 4718596
  107.5 140.9 %copy-start.4 = (f32[32]{0:T(128)S(1)}, f32[32]{0:T(128)}, u32[]{:S(2)}) copy-start(f32[32]{0:T(128)} %param.12) | copy-start | bytes 388
  244.7 13.8 %all-to-all-start.1 = ((bf16[48,2,4096]{2,0,1:T(8,128)(2,1)}), bf16[48,2,4096]{2,0,1:T(8,128)(2,1)S(1)}, u32[]{:S(2)}, u32[]{:S(2)}) async-start(bf16[48,2,4096]{2,0,1:T(8,128)(2,1)} %bitcast.53), calls=%async_computation.1 | async-start | bytes 1572864 | tf_op jit(solution)/shard_map/all_to_all | solution.py:64
  248.3 70.2 %all-gather.5.cloned.1.call-start = ((), (), s32[]{:S(2)}) async-start(), calls=%async_computation.7 | async-start | bytes 2359296 | tf_op jit(solution)/shard_map/all_gather | solution.py:55
  292.8 182.1 %reduce-scatter.9.cloned.1.call-start = ((), (), s32[]{:S(2)}) async-start(), calls=%async_computation.9 | async-start | bytes 13369344
  494.0 5.5 %copy-start.1 = (f32[128]{0:T(128)S(1)}, f32[128]{0:T(128)}, u32[]{:S(2)}) copy-start(f32[128]{0:T(128)} %param.13) | copy-start | bytes 1540
Sparse Core Ops, SparseCore 0:
  35.8 26.4 all-gather.2
  107.6 134.5 reduce-scatter.6
  292.9 25.4 all-gather.4
  340.3 134.5 reduce-scatter.8
where the time goes:
time: 507 us; the launch traced here: 506 us
  waiting for transfers between devices  324 us (64%)
  blocking collectives  65.3 us (13%)
  matrix products  53.8 us (11%)
  local copies, waits for them, and re-layouts  37.3 us (7%)
  between operations  13.3 us (3%)
  other arithmetic  8.42 us (2%)
    unnamed x6, waiting for transfers between devices  269 us
    all_to_all x2, blocking collectives, body(): lax.all_to_all(rounded, 'cd', split_axis=1, concat_axis=0, tiled=True)  52.5 us
    all_gather x2, waiting for transfers between devices, body(): lax.all_gather(regrouped, 'ab', axis=1, tiled=True)  51.9 us
    dot_general x2, matrix products, body(): lax.dot_general(lax.all_gather(regrouped, 'ab', axis=1, tiled=True), weig...  44.1 us
    unnamed x11, local copies, waits for them, and re-layouts  16.7 us
    convert_element_type x6, local copies, waits for them, and re-layouts, body(): flip_tiles(tiles, tile_width).astype(jnp.float32)  13.3 us
    all_to_all x1, blocking collectives, body(): lax.all_to_all(swapped.astype(jnp.bfloat16).reshape(rows_dev, ab_count, t...  12.7 us
  transfers between devices with their start and end apart: 5, of which 5 were waited for; matrix products, arithmetic and copies ran while one was open for 2% of the time, Pallas kernels for 0%

commit v1 on v0

v1 whole, which is shorter than its diff:
```python
import functools

import jax
import jax.numpy as jnp
from jax import lax
from jax.experimental import pallas as pl
from jax.experimental.pallas import tpu as pltpu
from jax.sharding import PartitionSpec as P

NV = 128
NOCC = 32
BLK = 128
ITERS = 2
STRIP = 16
MESH = pl.DeviceIdType.MESH
NT = (((1,), (1,)), ((), ()))


def flip_tiles(tiles, tile_width):
    row_count, tile_count = tiles.shape[:2]
    turned = jnp.swapaxes(tiles.reshape(row_count, tile_count, tile_width, tile_width), 2, 3)
    return turned.reshape(row_count, tile_count * tile_width * tile_width)


def bit_of(index, bit):
    return lax.rem(index // (1 << bit), 2)


def flip_bit(index, bit):
    return index + (1 - 2 * bit_of(index, bit)) * (1 << bit)


def ladder_kernel(
    bits, chunks, diag_chunks, width,
    low_ref, swap_ref, straight_ref, mirrored_ref, out_ref,
    straight, mirrored, *rest,
):
    held = rest[: bits + 1]
    load_sem, mirror_sem, send_sem, recv_sem = rest[bits + 1 :]
    ab = lax.axis_index("ab")
    cd = lax.axis_index("cd")
    rows = out_ref.shape[0]
    own = [bit_of(cd, bit) for bit in range(bits)]
    partner = [(ab, flip_bit(cd, bit)) for bit in range(bits)]

    def at(stage, chunk, which):
        lead = (slice(None),) * (bits - 1 - stage)
        return held[stage].at[(chunk,) + lead + (which,)]

    def copy(stage, chunk):
        return pltpu.make_async_remote_copy(
            src_ref=at(stage, chunk, 1 - own[stage]),
            dst_ref=held[stage + 1].at[chunk],
            send_sem=send_sem.at[stage, chunk],
            recv_sem=recv_sem.at[stage, chunk],
            device_id=partner[stage],
            device_id_type=MESH,
        )

    def load_straight(chunk):
        start = pl.multiple_of(chunk * width, width)
        return pltpu.make_async_copy(
            straight_ref.at[pl.ds(start, width)], straight.at[chunk], load_sem.at[chunk]
        )

    def load_mirrored(chunk):
        start = pl.multiple_of(chunk * width, width)
        return pltpu.make_async_copy(
            mirrored_ref.at[pl.ds(start, width)], mirrored.at[chunk], mirror_sem.at[chunk]
        )

    @pl.loop(0, diag_chunks)
    def _(chunk):
        load_straight(chunk).start()
        load_mirrored(chunk).start()

    @pl.loop(diag_chunks, chunks)
    def _(chunk):
        load_straight(chunk).start()

    barrier = pltpu.get_barrier_semaphore()
    for device in partner:
        pl.semaphore_signal(barrier, inc=1, device_id=device, device_id_type=MESH)
    pl.semaphore_wait(barrier, bits)

    def put(chunk, product):
        value = product.astype(jnp.bfloat16)
        for block in range(1 << bits):
            index = tuple((block >> (bits - 1 - axis)) & 1 for axis in range(bits))
            held[0][(chunk,) + index] = value[block * rows : (block + 1) * rows]

    @pl.loop(0, chunks + 2 * bits)
    def _(step):
        @pl.when(step < diag_chunks)
        def _():
            load_straight(step).wait()
            load_mirrored(step).wait()
            total = lax.dot_general(
                low_ref[...], straight[step], NT, preferred_element_type=jnp.float32
            )
            total += lax.dot_general(
                swap_ref[...], mirrored[step], NT, preferred_element_type=jnp.float32
            )
            put(step, total)
            copy(0, step).start()

        @pl.when((step >= diag_chunks) & (step < chunks))
        def _():
            load_straight(step).wait()
            put(
                step,
                lax.dot_general(
                    low_ref[...], straight[step], NT, preferred_element_type=jnp.float32
                ),
            )
            copy(0, step).start()

        for stage in range(bits):
            chunk = step - (2 * stage + 1)

            @pl.when((chunk >= 0) & (chunk < chunks))
            def _():
                copy(stage, chunk).wait_recv()
                mine = at(stage, chunk, own[stage])[...].astype(jnp.float32)
                total = held[stage + 1][chunk].astype(jnp.float32) + mine
                if stage < bits - 1:
                    held[stage + 1][chunk] = total.astype(jnp.bfloat16)
                    copy(stage + 1, chunk).start()
                else:
                    out_ref[:, pl.ds(pl.multiple_of(chunk * width, width), width)] = total

    @pl.loop(0, chunks)
    def _(chunk):
        for stage in range(bits):
            copy(stage, chunk).wait_send()


def ladder_sums(low, swapped, straight, mirrored, rows, width):
    count = low.shape[0] // rows
    bits = count.bit_length() - 1
    depth = low.shape[1]
    chunks = straight.shape[0] // width
    diag_chunks = mirrored.shape[0] // width
    held = [
        pltpu.VMEM((chunks,) + (2,) * (bits - stage) + (rows, width), jnp.bfloat16)
        for stage in range(bits + 1)
    ]
    return pl.pallas_call(
        functools.partial(ladder_kernel, bits, chunks, diag_chunks, width),
        out_shape=jax.ShapeDtypeStruct((rows, chunks * width), jnp.float32),
        in_specs=[pl.BlockSpec(memory_space=pltpu.VMEM)] * 2
        + [pl.BlockSpec(memory_space=pl.ANY)] * 2,
        out_specs=pl.BlockSpec(memory_space=pltpu.VMEM),
        scratch_shapes=[
            pltpu.VMEM((chunks, width, depth), jnp.bfloat16),
            pltpu.VMEM((diag_chunks, width, depth), jnp.bfloat16),
            *held,
            pltpu.SemaphoreType.DMA((chunks,)),
            pltpu.SemaphoreType.DMA((diag_chunks,)),
            pltpu.SemaphoreType.DMA((bits, chunks)),
            pltpu.SemaphoreType.DMA((bits, chunks)),
        ],
        compiler_params=pltpu.CompilerParams(
            collective_id=0, has_side_effects=True, vmem_limit_bytes=58 * 2**20
        ),
    )(low, swapped, straight, mirrored)


def body(amplitudes, driver, ladder, block_mask, pair_list, occ_energy, virt_energy):
    ab_count = lax.axis_size("ab")
    ab_index = lax.axis_index("ab")
    cd_index = lax.axis_index("cd")
    rows_dev, cols_dev = amplitudes.shape
    out_rows, in_cols = ladder.shape
    tile_width = NV // ab_count
    tile_area = tile_width * tile_width
    strip = min(STRIP, tile_width)
    strips = tile_width // strip
    diag_cols = sum(strip * (tile_width - s * strip) for s in range(strips))
    width = min(512, tile_area)

    weights = ladder.reshape(out_rows // BLK, BLK, in_cols // BLK, BLK)
    weights = (weights * block_mask.astype(jnp.bfloat16)[:, None, :, None]).reshape(
        ab_count, tile_width, tile_width, in_cols
    )
    diag_tile = lax.dynamic_index_in_dim(weights, ab_index, 0, keepdims=False)

    def pack(tile):
        return jnp.concatenate(
            [
                tile[s * strip : (s + 1) * strip, s * strip :].reshape(-1, in_cols)
                for s in range(strips)
            ]
        )

    others = [
        lax.dynamic_index_in_dim(
            weights, lax.rem(ab_index + j, ab_count), 0, keepdims=False
        ).reshape(tile_area, in_cols)
        for j in range(1, ab_count)
    ]
    straight = jnp.concatenate([pack(diag_tile)] + others)
    mirrored = pack(jnp.swapaxes(diag_tile, 0, 1))

    pairs_local = ab_index * cols_dev + jnp.arange(cols_dev, dtype=jnp.int32)
    big_a = pairs_local // (tile_width * NV)
    big_b = pairs_local // tile_area % ab_count
    first = big_a * tile_width + pairs_local // tile_width % tile_width
    second = big_b * tile_width + pairs_local % tile_width
    virt_index = jnp.arange(NV, dtype=jnp.int32)
    picks = (first[:, None] == virt_index).astype(jnp.float32) + (
        second[:, None] == virt_index
    ).astype(jnp.float32)
    col_energy = jnp.dot(picks, virt_energy, precision=lax.Precision.HIGHEST)
    row_pairs = lax.dynamic_slice_in_dim(pair_list, cd_index * rows_dev, rows_dev)
    occ_index = jnp.arange(NOCC, dtype=jnp.int32)
    occ_picks = (row_pairs[:, None] // NOCC == occ_index).astype(jnp.float32)
    occ_picks = occ_picks + (row_pairs[:, None] % NOCC == occ_index).astype(jnp.float32)
    row_energy = jnp.dot(occ_picks, occ_energy, precision=lax.Precision.HIGHEST)
    denominator = col_energy[None, :] - row_energy[:, None]

    def swap_matrix(listed):
        diagonal = listed // NOCC == listed % NOCC
        index = jnp.arange(listed.shape[0], dtype=jnp.int32)
        mirror_row = jnp.where(diagonal, index, index ^ 1)
        return (mirror_row[:, None] == index).astype(jnp.bfloat16)

    row_swap = swap_matrix(row_pairs)
    all_swap = swap_matrix(pair_list)

    def spread(packed):
        pieces, start = [], 0
        for s in range(strips):
            wide = tile_width - s * strip
            piece = packed[:, start : start + strip * wide].reshape(rows_dev, strip, wide)
            start += strip * wide
            piece = jnp.concatenate([0.5 * piece[:, :, :strip], piece[:, :, strip:]], axis=2)
            pieces.append(jnp.pad(piece, ((0, 0), (0, 0), (s * strip, 0))))
        return jnp.concatenate(pieces, axis=1).reshape(rows_dev, tile_area)

    state = amplitudes
    for step in range(ITERS):
        rounded = state.astype(jnp.bfloat16)
        regrouped = lax.all_to_all(rounded, "cd", split_axis=1, concat_axis=0, tiled=True)
        low = lax.all_gather(regrouped, "ab", axis=1, tiled=True)
        swapped_low = jnp.dot(all_swap, low, preferred_element_type=jnp.float32)
        sums = ladder_sums(
            low, swapped_low.astype(jnp.bfloat16), straight, mirrored, rows_dev, width
        )
        parts = [spread(sums[:, :diag_cols])]
        for j in range(1, ab_count):
            start = diag_cols + (j - 1) * tile_area
            parts.append(sums[:, start : start + tile_area])
        placed = jnp.concatenate(parts, axis=1)
        received = jnp.roll(placed.reshape(rows_dev, ab_count, tile_area), ab_index, axis=1)
        received = received.reshape(rows_dev, cols_dev)
        swapped = jnp.dot(
            row_swap, received.astype(jnp.bfloat16), preferred_element_type=jnp.float32
        )
        tiles = lax.all_to_all(
            swapped.astype(jnp.bfloat16).reshape(rows_dev, ab_count, tile_area),
            "ab",
            split_axis=1,
            concat_axis=1,
            tiled=True,
        )
        symmetric = received + flip_tiles(tiles, tile_width).astype(jnp.float32)
        state = (driver + symmetric) / denominator
    return state


def solution(mesh):
    placed = (P("cd", "ab"), P("cd", "ab"), P("ab", "cd"), P("ab", "cd"), P(), P(), P())
    return jax.shard_map(body, mesh=mesh, in_specs=placed, out_specs=P("cd", "ab"), check_vma=False)
```

time: 507 us -> 392 us (0.77)
  waiting for transfers between devices: 324 us -> 36.8 us
  Pallas kernels: 0 us -> 152 us
  local copies, waits for them, and re-layouts: 37.3 us -> 91.5 us
  matrix products: 53.8 us -> 15.5 us
  blocking collectives: 65.3 us -> 36.8 us
  other arithmetic: 8.42 us -> 33.1 us
  starting transfers between devices: 3.84 us -> 11 us
    unnamed x6 -> x2, waiting for transfers between devices: 269 us -> 0.03 us
    pallas_call x0 -> x2, Pallas kernels: none -> 152 us  [ladder_sums(): pl.pallas_call(functools.partial(ladder_kernel, bits, chunks, diag_chunks...]
    dot_general x4, matrix products: 47.2 us -> 8.78 us  [the longest x2 7.97 us: body(): swapped_low = jnp.dot(all_swap, low, preferred_element_type=jnp.float32)]
    all_to_all x2 -> x1, blocking collectives: 52.5 us -> 23.5 us  [body(): lax.all_to_all(rounded, 'cd', split_axis=1, concat_axis=0, tiled=True)]
    slice x0 -> x27, local copies, waits for them, and re-layouts: none -> 24.5 us  [the longest x11 23.6 us: pack(): tile[s * strip:(s + 1) * strip, s * strip:].reshape(-1, in_cols)]
    dynamic_slice x0 -> x2, local copies, waits for them, and re-layouts: none -> 18.9 us  [the longest x1 11.3 us: body(): diag_tile = lax.dynamic_index_in_dim(weights, ab_index, 0, keepdims=False)]
    all_gather x2, waiting for transfers between devices: 51.9 us -> 33.7 us  [body(): low = lax.all_gather(regrouped, 'ab', axis=1, tiled=True)]
    concatenate x0 -> x5, local copies, waits for them, and re-layouts: none -> 12.9 us  [the longest x1 7.67 us: body(): straight = jnp.concatenate([pack(diag_tile)] + others)]
  transfers between devices with their start and end apart: 5 -> 4, of which waited for: 5 -> 3; matrix products, arithmetic and copies ran while one was open for 2% -> 21% of each run, Pallas kernels for 0% -> 0%
where the time goes in v1:
time: 392 us; the launch traced here: 390 us
  Pallas kernels  152 us (39%)
  local copies, waits for them, and re-layouts  91.5 us (23%)
  waiting for transfers between devices  36.8 us (9%)
  blocking collectives  36.8 us (9%)
  other arithmetic  33.1 us (8%)
  matrix products  15.5 us (4%)
  between operations  13.9 us (4%)
  starting transfers between devices  11 us (3%)
    pallas_call x2, Pallas kernels, ladder_sums(): pl.pallas_call(functools.partial(ladder_kernel, bits, chunks, diag_chunks...  152 us
    all_gather x2, waiting for transfers between devices, body(): low = lax.all_gather(regrouped, 'ab', axis=1, tiled=True)  33.7 us
    slice x11, local copies, waits for them, and re-layouts, pack(): tile[s * strip:(s + 1) * strip, s * strip:].reshape(-1, in_cols)  23.6 us
    all_to_all x1, blocking collectives, body(): lax.all_to_all(rounded, 'cd', split_axis=1, concat_axis=0, tiled=True)  23.5 us
    convert_element_type x6, local copies, waits for them, and re-layouts, body(): symmetric = received + flip_tiles(tiles, tile_width).astype(jnp.float32)  19.8 us
    all_to_all x1, blocking collectives, body(): lax.all_to_all(swapped.astype(jnp.bfloat16).reshape(rows_dev, ab_count, t...  13.3 us
    dynamic_slice x1, local copies, waits for them, and re-layouts, body(): diag_tile = lax.dynamic_index_in_dim(weights, ab_index, 0, keepdims=False)  11.3 us
    concatenate x1, other arithmetic, pack(): jnp.concatenate([tile[s * strip:(s + 1) * strip, s * strip:].reshape(-1,...  11.1 us
  transfers between devices with their start and end apart: 4, of which 3 were waited for; matrix products, arithmetic and copies ran while one was open for 21% of the time, Pallas kernels for 0%

profile of v1, /device:TPU:0, one launch (start us, length us, event | category | flops | bytes accessed | tf_op | source)
XLA Modules:
  0.0 390.4 jit_solution(10551851932686954242)
XLA Ops:
  9.1 7.4 %all-to-all-start = ((bf16[48,16,512]{2,0,1:T(8,128)(2,1)}), bf16[48,16,512]{2,0,1:T(8,128)(2,1)}, u32[]{:S(2)}, u32[]{:S(2)}) async-start(bf16[48,16,512]{2,0,1:T(8,128)(2,1)} %bitcast.72), calls=%async_computation | async-start | bytes 1572864 | tf_op jit(solution)/shard_map/all_to_all | solution.py:244
  16.9 8.0 %broadcast_multiply_fusion = bf16[2,64,64,1024]{3,2,1,0:T(8,128)(2,1)S(1)} fusion(bf16[2,64,64,1024]{3,2,1,0:T(8,128)(2,1)} %bitcast.81, bf16[2,64,1024]{2,1,0:T(8,128)(2,1)S(1)} %mul.64), kind=kLoop, calls=%fused_computation.2 | loop fusion | flops 8388608 | bytes 33816576 | tf_op jit(solution)/shard_map/mul | solution.py:183
  25.0 7.6 %constant_dynamic-slice_fusion.1 = (bf16[1,64,64,1024]{3,2,1,0:T(8,128)(2,1)}, bf16[1,64,64,1024]{3,2,1,0:T(8,128)(2,1)}) fusion(bf16[2,64,64,1024]{3,2,1,0:T(8,128)(2,1)S(1)} %broadcast_multiply_fusion, s32[]{:T(128)S(6)} %select_n.110, s32[]{:T(128)S(6)} %select_n.109), kind=kLoop, calls=%fused_computation.127 | loop fusion | bytes 33554440 | tf_op jit(solution)/shard_map/jit(dynamic_index_in_dim)/dynamic_slice | solution.py:197
  32.6 3.2 copy-done.1
  35.7 11.3 %copy.61 = bf16[1,64,64,1024]{3,1,2,0:T(8,128)(2,1)} copy(bf16[1,64,64,1024]{3,2,1,0:T(8,128)(2,1)} %get-tuple-element.10) | data formatting | bytes 16777216 | tf_op jit(solution)/shard_map/jit(dynamic_index_in_dim)/dynamic_slice | solution.py:186
  78.1 11.1 %pad_maximum_fusion.mirrored_ref = bf16[2560,1024]{1,0:T(8,128)(2,1)} fusion(bf16[256,1024]{1,0:T(8,128)(2,1)} %bitcast.101, bf16[512,1024]{1,0:T(8,128)(2,1)S(1)} %bitcast.92, bf16[768,1024]{1,0:T(8,128)(2,1)} %bitcast.90, bf16[1024,1024]{1,0:T(8,128)(2,1)S(1)} %bitcast.88), kind=kLoop, calls=%fused_computation.5 | loop fusion | flops 20971520 | bytes 10485760 | tf_op jit(solution)/shard_map/concatenate | solution.py:189
  89.2 7.7 %constant_dynamic-update-slice_fusion.straight_ref = bf16[6656,1024]{1,0:T(8,128)(2,1)} fusion(bf16[6656,1024]{1,0:T(8,128)(2,1)} %constant_dynamic-update-slice_fusion.1, bf16[4096,1024]{1,0:T(8,128)(2,1)} %bitcast.73), kind=kLoop, calls=%fused_computation.109 | loop fusion | bytes 16777216 | tf_op jit(solution)/shard_map/concatenate | solution.py:202
  96.9 8.0 %all-gather.3.cloned.1.call-done.low_ref = bf16[768,1024]{1,0:T(8,128)(2,1)} async-done(((bf16[768,512]{1,0:T(8,128)(2,1)}), bf16[768,1024]{1,0:T(8,128)(2,1)}) %all-gather.3.cloned.1.call-update) | async-done | bytes 1572880 | tf_op jit(solution)/shard_map/all_gather | solution.py:245
  104.9 4.0 %fusion.8.swap_ref = bf16[768,1024]{1,0:T(8,128)(2,1)} fusion(bf16[768,1024]{1,0:T(8,128)(2,1)} %all-gather.3.cloned.1.call-done.low_ref, s32[768]{0:T(1024)S(1)} %xor_select_fusion), kind=kOutput, calls=%fused_computation.27 | convolution fusion | flops 1209335808 | bytes 3148800 | tf_op jit(solution)/shard_map/dot_general | solution.py:246
  108.9 75.8 %shard_map.73 = f32[48,6656]{1,0:T(8,128)} custom-call(bf16[768,1024]{1,0:T(8,128)(2,1)} %all-gather.3.cloned.1.call-done.low_ref, bf16[768,1024]{1,0:T(8,128)(2,1)} %fusion.8.swap_ref, bf16[6656,1024]{1,0:T(8,128)(2,1)} %constant_dynamic-update-slice_fusion.straight_ref, bf16[2560,1024]{1,0:T(8,128)(2,1)} %pad_maximum_fusion.mirrored_ref), custom_call_target="tpu_custom_call" | custom-call | tf_op jit(solution)/shard_map/pallas_call | solution.py:148
  191.5 3.5 all-to-all-start.1
  195.5 6.5 %fusion = f32[1,8192]{1,0:T(1,128)S(1)} fusion(s32[8192]{0:T(1024)S(1)} %get-tuple-element.20, s32[8192]{0:T(1024)S(1)} %get-tuple-element.19, f32[128]{0:T(128)S(1)} %copy-done), kind=kOutput, calls=%fused_computation.6 | convolution fusion | flops 17825792 | bytes 98816 | tf_op jit(solution)/shard_map/dot_general | solution.py:214
  202.0 3.1 all-to-all-done.1
  207.6 3.5 copy.42
  211.1 3.4 reshape.229
  216.5 23.5 %all_to_all.48 = bf16[48,16,512]{2,0,1:T(8,128)(2,1)} all-to-all(bf16[48,16,512]{2,0,1:T(8,128)(2,1)S(1)} %bitcast.97), channel_id=1, replica_groups=mesh['ab'=2,'cd'=16] {'cd'}, dimensions={1} | all-to-all | bytes 1572864 | tf_op jit(solution)/shard_map/all_to_all | solution.py:244
  240.1 25.7 %all-gather.5.cloned.1.call-done.low_ref = bf16[768,1024]{1,0:T(8,128)(2,1)} async-done(((bf16[768,512]{1,0:T(8,128)(2,1)}), bf16[768,1024]{1,0:T(8,128)(2,1)}) %all-gather.5.cloned.1.call-update) | async-done | bytes 1572880 | tf_op jit(solution)/shard_map/all_gather | solution.py:245
  265.7 4.0 %fusion.9.swap_ref = bf16[768,1024]{1,0:T(8,128)(2,1)} fusion(bf16[768,1024]{1,0:T(8,128)(2,1)} %all-gather.5.cloned.1.call-done.low_ref, s32[768]{0:T(1024)S(1)} %xor_select_fusion), kind=kOutput, calls=%fused_computation.28 | convolution fusion | flops 1209335808 | bytes 3148800 | tf_op jit(solution)/shard_map/dot_general | solution.py:246
  269.7 75.8 %shard_map.74 = f32[48,6656]{1,0:T(8,128)} custom-call(bf16[768,1024]{1,0:T(8,128)(2,1)} %all-gather.5.cloned.1.call-done.low_ref, bf16[768,1024]{1,0:T(8,128)(2,1)} %fusion.9.swap_ref, bf16[6656,1024]{1,0:T(8,128)(2,1)} %constant_dynamic-update-slice_fusion.straight_ref, bf16[2560,1024]{1,0:T(8,128)(2,1)} %pad_maximum_fusion.mirrored_ref), custom_call_target="tpu_custom_call" | custom-call | tf_op jit(solution)/shard_map/pallas_call | solution.py:148
  356.7 13.3 %all_to_all.49 = bf16[48,2,4096]{2,0,1:T(8,128)(2,1)} all-to-all(bf16[48,2,4096]{2,0,1:T(8,128)(2,1)S(1)} %bitcast.98), channel_id=1, replica_groups=mesh['ab'=2,'cd'=16] {'ab'}, dimensions={1} | all-to-all | bytes 1572864 | tf_op jit(solution)/shard_map/all_to_all | solution.py:260
  370.0 3.6 reshape.232
  373.6 3.6 copy.48
  377.2 3.3 reshape.230
  380.5 3.0 subtract_divide_fusion
  (113 shorter events, 56.4 us)
Async XLA Ops:
  6.5 188.9 %copy-start = (f32[128]{0:T(128)S(1)}, f32[128]{0:T(128)}, u32[]{:S(2)}) copy-start(f32[128]{0:T(128)} %param.15) | copy-start | bytes 1540
  8.0 8.5 %copy-start.11 = (s32[64,8]{0,1:T(8,128)S(1)}, s32[64,8]{0,1:T(8,128)}, u32[]{:S(2)}) copy-start(s32[64,8]{0,1:T(8,128)} %param.12) | copy-start | bytes 6148
  9.1 67.1 %all-to-all-start = ((bf16[48,16,512]{2,0,1:T(8,128)(2,1)}), bf16[48,16,512]{2,0,1:T(8,128)(2,1)}, u32[]{:S(2)}, u32[]{:S(2)}) async-start(bf16[48,16,512]{2,0,1:T(8,128)(2,1)} %bitcast.72), calls=%async_computation | async-start | bytes 1572864 | tf_op jit(solution)/shard_map/all_to_all | solution.py:244
  16.5 88.4 %all-gather.3.cloned.1.call-start = ((), (), s32[]{:S(2)}) async-start(), calls=%async_computation.4 | async-start | bytes 2359296 | tf_op jit(solution)/shard_map/all_gather | solution.py:245
  24.9 10.8 %copy-start.1 = (bf16[2,64,64,1024]{3,2,1,0:T(8,128)(2,1)}, bf16[2,64,64,1024]{3,2,1,0:T(8,128)(2,1)S(1)}, u32[]{:S(2)}) copy-start(bf16[2,64,64,1024]{3,2,1,0:T(8,128)(2,1)S(1)} %broadcast_multiply_fusion) | copy-start | bytes 50331652
  61.9 5.0 %copy-start.2 = (bf16[16,48,1024]{2,0,1:T(8,128)(2,1)S(1)}, bf16[16,48,1024]{2,0,1:T(8,128)(2,1)}, u32[]{:S(2)}) copy-start(bf16[16,48,1024]{2,0,1:T(8,128)(2,1)} %slice.131) | copy-start | bytes 4718596
  66.9 2.0 copy-start.10
  71.4 2.1 copy-start.3
  73.5 1.7 copy-start.5
  184.7 2.1 slice-start.4
  185.5 1.6 slice-start.5
  190.6 4.7 %copy-start.12 = (s32[48]{0:T(128)S(1)}, s32[48]{0:T(128)}, u32[]{:S(2)}) copy-start(s32[48]{0:T(128)} %get-tuple-element.7) | copy-start | bytes 580
  190.6 4.7 %copy-start.13 = (s32[48]{0:T(128)S(1)}, s32[48]{0:T(128)}, u32[]{:S(2)}) copy-start(s32[48]{0:T(128)} %get-tuple-element.8) | copy-start | bytes 580
  190.6 4.7 %copy-start.14 = (f32[32]{0:T(128)S(1)}, f32[32]{0:T(128)}, u32[]{:S(2)}) copy-start(f32[32]{0:T(128)} %param.14) | copy-start | bytes 388
  191.5 13.6 %all-to-all-start.1 = ((bf16[48,2,4096]{2,0,1:T(8,128)(2,1)}), bf16[48,2,4096]{2,0,1:T(8,128)(2,1)S(1)}, u32[]{:S(2)}, u32[]{:S(2)}) async-start(bf16[48,2,4096]{2,0,1:T(8,128)(2,1)} %bitcast.71), calls=%async_computation.1 | async-start | bytes 1572864 | tf_op jit(solution)/shard_map/all_to_all | solution.py:260
  195.1 70.7 %all-gather.5.cloned.1.call-start = ((), (), s32[]{:S(2)}) async-start(), calls=%async_computation.5 | async-start | bytes 2359296 | tf_op jit(solution)/shard_map/all_gather | solution.py:245
  202.0 12.5 %copy-start.8 = (f32[1,8192]{1,0:T(1,128)}, f32[1,8192]{1,0:T(1,128)S(1)}, u32[]{:S(2)}) copy-start(f32[1,8192]{1,0:T(1,128)S(1)} %fusion) | copy-start | bytes 98308
  211.1 3.4 copy-start.4
  345.5 3.0 slice-start.1
  346.4 2.5 slice-start.2
  348.9 2.1 slice-start
  351.4 1.0 copy-start.6
  351.4 1.1 copy-start.7
  377.2 3.3 copy-start.9
  (1 other events, 0.9 us)
Sparse Core Ops, SparseCore 0:
  76.3 28.5 all-gather.2
  240.2 25.4 all-gather.4

commit v2 on v1

--- a/solution.py
+++ b/solution.py
@@ -166,6 +166,325 @@
     )(low, swapped, straight, mirrored)
 
 
+def iteration_kernel(
+    bits, width, strip, rows, half,
+    state_ref, diagonal_ref, weight_ref, turned_ref, sums_ref, other_ref,
+    low, straight, mirrored, outer, part, part_y, *rest,
+):
+    held = (part,) + rest[:bits]
+    final, landed = rest[bits : bits + 2]
+    (
+        load_sem, self_sem, a_send, a_recv, b_send, b_recv,
+        core_send, core_recv, y_send, y_recv, send_sem, recv_sem, last_send, last_recv,
+    ) = rest[bits + 2 :]
+    ab = lax.axis_index("ab")
+    cd = lax.axis_index("cd")
+    count = 1 << bits
+    tile_width = weight_ref.shape[1]
+    depth = weight_ref.shape[3]
+    piece = depth // 2
+    keeps = outer.shape[0] // (2 * width)
+    diags = keeps + 1
+    products = 3 * keeps + 1
+    finals = diags + keeps
+    own = [bit_of(cd, bit) for bit in range(bits)]
+    partner = [(ab, flip_bit(cd, bit)) for bit in range(bits)]
+    across = (1 - ab, cd)
+
+    def remote(src, dst, send, recv, device):
+        return pltpu.make_async_remote_copy(
+            src_ref=src, dst_ref=dst, send_sem=send, recv_sem=recv,
+            device_id=device, device_id_type=MESH,
+        )
+
+    for s in range(tile_width // strip):
+        wide = tile_width - s * strip
+        base = sum(strip * (tile_width - r * strip) for r in range(s))
+
+        @pl.loop(0, strip)
+        def _(x):
+            rows_to = pl.ds(pl.multiple_of(base + x * wide, strip), wide)
+            rows_from = pl.ds(s * strip, wide)
+            pltpu.make_async_copy(
+                weight_ref.at[ab, s * strip + x, rows_from], straight.at[rows_to], load_sem.at[0]
+            ).start()
+            pltpu.make_async_copy(
+                turned_ref.at[ab, s * strip + x, rows_from], mirrored.at[rows_to], load_sem.at[1]
+            ).start()
+
+    @pl.loop(0, tile_width)
+    def _(x):
+        side = lax.rem(x // half + ab, 2)
+        kept = pl.ds(pl.multiple_of(side * half, half), half)
+        sent = pl.ds(pl.multiple_of((1 - side) * half, half), half)
+        to = pl.multiple_of(x * half, half)
+        pltpu.make_async_copy(
+            weight_ref.at[1 - ab, x, kept], outer.at[pl.ds(to, half)], load_sem.at[2]
+        ).start()
+        pltpu.make_async_copy(
+            turned_ref.at[1 - ab, x, sent],
+            outer.at[pl.ds(to + tile_width * half, half)],
+            load_sem.at[2],
+        ).start()
+
+    barrier = pltpu.get_barrier_semaphore()
+
+    @pl.loop(1, count)
+    def _(j):
+        pl.semaphore_signal(
+            barrier, inc=1, device_id=(ab, lax.rem(cd + j, count)), device_id_type=MESH
+        )
+
+    pl.semaphore_signal(barrier, inc=1, device_id=across, device_id_type=MESH)
+    pl.semaphore_wait(barrier, count)
+
+    def rows_of(source):
+        return pl.ds(pl.multiple_of(source * rows, rows), rows)
+
+    def cols_of(side):
+        return pl.ds(pl.multiple_of(side * piece, piece), piece)
+
+    def scatter(target, source):
+        return remote(
+            state_ref.at[:, pl.ds(pl.multiple_of(target * piece, piece), piece)],
+            low.at[0, rows_of(source), cols_of(ab)],
+            a_send.at[target], a_recv.at[source], (ab, target),
+        )
+
+    def forward(source, side):
+        block = low.at[0, rows_of(source), cols_of(side)]
+        return remote(block, block, b_send.at[source], b_recv.at[source], across)
+
+    stay = pltpu.make_async_copy(
+        state_ref.at[:, pl.ds(pl.multiple_of(cd * piece, piece), piece)],
+        low.at[0, rows_of(cd), cols_of(ab)],
+        self_sem,
+    )
+    stay.start()
+
+    @pl.loop(0, count)
+    def _(i):
+        j = lax.rem(i + count // 2, count)
+
+        @pl.when(j != 0)
+        def _():
+            scatter(lax.rem(cd + j, count), cd).start()
+
+    stay.wait()
+    forward(cd, ab).start()
+
+    @pl.loop(0, count)
+    def _(i):
+        j = lax.rem(i + count // 2, count)
+
+        @pl.when(j != 0)
+        def _():
+            source = lax.rem(cd + count - j, count)
+            scatter(cd, source).wait_recv()
+            forward(source, ab).start()
+
+    pltpu.make_async_copy(straight, straight, load_sem.at[0]).wait()
+    pltpu.make_async_copy(mirrored, mirrored, load_sem.at[1]).wait()
+    pltpu.make_async_copy(outer, outer, load_sem.at[2]).wait()
+
+    @pl.loop(0, count)
+    def _(i):
+        j = lax.rem(i + count // 2, count)
+        source = lax.rem(cd + count - j, count)
+        forward(source, 1 - ab).wait_recv()
+
+    odd = lax.rem(lax.broadcasted_iota(jnp.int32, (rows, 128), 0), 2) == 1
+
+    @pl.loop(0, count)
+    def _(source):
+        at = rows_of(source)
+        same = diagonal_ref[at, :] != 0
+        for lane in range(0, depth, 128):
+            value = low[0, at, lane : lane + 128].astype(jnp.float32)
+            other = jnp.where(odd, pltpu.roll(value, 1, 0), pltpu.roll(value, rows - 1, 0))
+            low[1, at, lane : lane + 128] = jnp.where(same, value, other).astype(jnp.bfloat16)
+
+    def at(stage, index, which):
+        lead = (slice(None),) * (bits - 1 - stage)
+        return held[stage].at[(index,) + lead + (which,)]
+
+    def place(q):
+        turn = q // 2
+        diag = jnp.where(turn == keeps, 3 * keeps, 3 * turn + 1)
+        return jnp.where(lax.rem(q, 2) == 0, diag, 3 * turn + 2)
+
+    def core_copy(u):
+        return remote(
+            at(0, u, 1 - own[0]), held[1].at[u], core_send.at[u], core_recv.at[u], partner[0]
+        )
+
+    def y_copy(j):
+        return remote(held[1].at[3 * j], part_y.at[j], y_send.at[j], y_recv.at[j], across)
+
+    def stage_copy(stage, q):
+        source = at(1, place(q), 1 - own[1]) if stage == 1 else at(stage, q, 1 - own[stage])
+        return remote(
+            source, held[stage + 1].at[q],
+            send_sem.at[stage - 1, q], recv_sem.at[stage - 1, q], partner[stage],
+        )
+
+    def last_copy(j):
+        return remote(final.at[j], landed.at[j], last_send.at[j], last_recv.at[j], across)
+
+    def put(u, product):
+        value = product.astype(jnp.bfloat16)
+        for block in range(count):
+            index = tuple((block >> (bits - 1 - axis)) & 1 for axis in range(bits))
+            part[(u,) + index] = value[block * rows : (block + 1) * rows]
+
+    def rows_at(start):
+        return pl.ds(pl.multiple_of(start, width), width)
+
+    def dot(left, right):
+        return lax.dot_general(left, right, NT, preferred_element_type=jnp.float32)
+
+    y_lag = 7
+    lags = [5 + 2 * s for s in range(bits - 1)]
+
+    @pl.loop(0, 2 * (finals - 1) + lags[-1] + 1)
+    def _(step):
+        turn = step // 3
+        kind = lax.rem(step, 3)
+        is_diag = ((kind == 1) & (step < 3 * keeps)) | (step == 3 * keeps)
+
+        @pl.when(is_diag)
+        def _():
+            total = dot(low[0], straight[rows_at(turn * width)])
+            put(step, total + dot(low[1], mirrored[rows_at(turn * width)]))
+            core_copy(step).start()
+
+        @pl.when((kind != 1) & (step < 3 * keeps))
+        def _():
+            sent = 1 - kind // 2
+            put(step, dot(low[sent], outer[rows_at((sent * keeps + turn) * width)]))
+            core_copy(step).start()
+
+        u = step - 1
+
+        @pl.when((u >= 0) & (u < products))
+        def _():
+            core_copy(u).wait_recv()
+            held[1][u] = held[1][u] + at(0, u, own[0])[...]
+            u_kind = lax.rem(u, 3)
+
+            @pl.when((u_kind == 1) | (u == 3 * keeps))
+            def _():
+                stage_copy(1, 2 * (u // 3)).start()
+
+            @pl.when((u_kind == 0) & (u < 3 * keeps))
+            def _():
+                y_copy(u // 3).start()
+
+        v = step - y_lag
+
+        @pl.when((v >= 0) & (lax.rem(v + 3, 3) == 0) & (v < 3 * keeps))
+        def _():
+            y_copy(v // 3).wait_recv()
+            held[1][v + 2] = held[1][v + 2] + part_y[v // 3]
+            stage_copy(1, 2 * (v // 3) + 1).start()
+
+        for stage in range(1, bits):
+            w = step - lags[stage - 1]
+            q = w // 2
+
+            @pl.when((w >= 0) & (lax.rem(w + 2, 2) == 0) & (q < finals))
+            def _():
+                stage_copy(stage, q).wait_recv()
+                index = place(q) if stage == 1 else q
+                mine = at(stage, index, own[stage])[...]
+                if stage < bits - 1:
+                    held[stage + 1][q] = held[stage + 1][q] + mine
+                    stage_copy(stage + 1, q).start()
+                else:
+                    total = held[stage + 1][q].astype(jnp.float32) + mine.astype(jnp.float32)
+                    kept = lax.rem(q, 2) == 1
+                    start = jnp.where(kept, diags + q // 2, q // 2) * width
+                    sums_ref[:, rows_at(start)] = total
+
+                    @pl.when(kept)
+                    def _():
+                        final[q // 2] = total.astype(jnp.bfloat16)
+                        last_copy(q // 2).start()
+
+    for j in range(keeps):
+        last_copy(j).wait_recv()
+        other_ref[:, j * width : (j + 1) * width] = landed[j]
+
+    @pl.loop(0, count)
+    def _(i):
+        @pl.when(i != cd)
+        def _():
+            scatter(i, cd).wait_send()
+
+        forward(i, ab).wait_send()
+
+    @pl.loop(0, products)
+    def _(u):
+        core_copy(u).wait_send()
+
+    @pl.loop(0, keeps)
+    def _(j):
+        y_copy(j).wait_send()
+        last_copy(j).wait_send()
+
+    @pl.loop(0, finals)
+    def _(q):
+        for stage in range(1, bits):
+            stage_copy(stage, q).wait_send()
+
+
+def iteration_sums(state, diagonal, weights, turned, width, strip):
+    rows = state.shape[0]
+    count = diagonal.shape[0] // rows
+    bits = count.bit_length() - 1
+    tile_width, depth = weights.shape[1], weights.shape[3]
+    half = tile_width // 2
+    diag_cols = sum(
+        strip * (tile_width - s * strip) for s in range(tile_width // strip)
+    )
+    keeps = tile_width * half // width
+    products, finals = 3 * keeps + 1, 2 * keeps + 1
+    dma = pltpu.SemaphoreType.DMA
+    block = (rows, width)
+    return pl.pallas_call(
+        functools.partial(iteration_kernel, bits, width, strip, rows, half),
+        out_shape=(
+            jax.ShapeDtypeStruct((rows, finals * width), jnp.float32),
+            jax.ShapeDtypeStruct((rows, keeps * width), jnp.bfloat16),
+        ),
+        in_specs=[pl.BlockSpec(memory_space=pltpu.VMEM)] * 2
+        + [pl.BlockSpec(memory_space=pl.ANY)] * 2,
+        out_specs=[pl.BlockSpec(memory_space=pltpu.VMEM)] * 2,
+        scratch_shapes=[
+            pltpu.VMEM((2, count * rows, depth), jnp.bfloat16),
+            pltpu.VMEM((diag_cols, depth), jnp.bfloat16),
+            pltpu.VMEM((diag_cols, depth), jnp.bfloat16),
+            pltpu.VMEM((2 * tile_width * half, depth), jnp.bfloat16),
+            pltpu.VMEM((products,) + (2,) * bits + block, jnp.bfloat16),
+            pltpu.VMEM((keeps,) + (2,) * (bits - 1) + block, jnp.bfloat16),
+            pltpu.VMEM((products,) + (2,) * (bits - 1) + block, jnp.bfloat16),
+            *[
+                pltpu.VMEM((finals,) + (2,) * (bits - 1 - s) + block, jnp.bfloat16)
+                for s in range(1, bits)
+            ],
+            pltpu.VMEM((keeps,) + block, jnp.bfloat16),
+            pltpu.VMEM((keeps,) + block, jnp.bfloat16),
+            dma((3,)), dma,
+            dma((count,)), dma((count,)), dma((count,)), dma((count,)),
+            dma((products,)), dma((products,)), dma((keeps,)), dma((keeps,)),
+            dma((bits - 1, finals)), dma((bits - 1, finals)), dma((keeps,)), dma((keeps,)),
+        ],
+        compiler_params=pltpu.CompilerParams(
+            collective_id=1, has_side_effects=True, vmem_limit_bytes=60 * 2**20
+        ),
+    )(state, diagonal, weights, turned)
+
+
 def body(amplitudes, driver, ladder, block_mask, pair_list, occ_energy, virt_energy):
     ab_count = lax.axis_size("ab")
     ab_index = lax.axis_index("ab")
@@ -183,6 +502,12 @@
     weights = (weights * block_mask.astype(jnp.bfloat16)[:, None, :, None]).reshape(
         ab_count, tile_width, tile_width, in_cols
     )
+    paired = (
+        ab_count == 2
+        and tile_area % (2 * width) == 0
+        and diag_cols == (tile_area // 2 // width + 1) * width
+    )
+    turned = jnp.swapaxes(weights, 1, 2)
     diag_tile = lax.dynamic_index_in_dim(weights, ab_index, 0, keepdims=False)
 
     def pack(tile):
@@ -238,9 +563,49 @@
             pieces.append(jnp.pad(piece, ((0, 0), (0, 0), (s * strip, 0))))
         return jnp.concatenate(pieces, axis=1).reshape(rows_dev, tile_area)
 
+    diag_rows = (pair_list // NOCC == pair_list % NOCC).astype(jnp.float32)
+    diag_rows = jnp.broadcast_to(diag_rows[:, None], (pair_list.shape[0], 128))
+    odd_row = (jnp.arange(rows_dev) % 2 == 1)[:, None]
+    same_row = (row_pairs // NOCC == row_pairs % NOCC)[:, None]
+
+    def swap_rows(value):
+        above = jnp.concatenate([value[-1:], value[:-1]])
+        below = jnp.concatenate([value[1:], value[:1]])
+        return jnp.where(same_row, value, jnp.where(odd_row, above, below))
+
+    def symmetric_tiles(sums, other):
+        half = tile_width // 2
+        diag = spread(sums[:, :diag_cols])
+        diag = diag + flip_tiles(swap_rows(diag)[:, None, :], tile_width)
+        kept = sums[:, diag_cols:].reshape(rows_dev, 2, half, half)
+        came = swap_rows(other).reshape(rows_dev, 2, half, half).swapaxes(2, 3)
+        came = jnp.where(ab_index == 1, came, came[:, ::-1]).astype(jnp.float32)
+        first_half = jnp.concatenate(
+            [
+                jnp.where(ab_index == 0, kept[:, 0], came[:, 0]),
+                jnp.where(ab_index == 0, came[:, 0], kept[:, 0]),
+            ],
+            axis=2,
+        )
+        second_half = jnp.concatenate(
+            [
+                jnp.where(ab_index == 0, came[:, 1], kept[:, 1]),
+                jnp.where(ab_index == 0, kept[:, 1], came[:, 1]),
+            ],
+            axis=2,
+        )
+        off = jnp.concatenate([first_half, second_half], axis=1).reshape(rows_dev, tile_area)
+        return jnp.concatenate(
+            [jnp.where(ab_index == 0, diag, off), jnp.where(ab_index == 0, off, diag)], axis=1
+        )
+
     state = amplitudes
     for step in range(ITERS):
         rounded = state.astype(jnp.bfloat16)
+        if paired:
+            sums, other = iteration_sums(rounded, diag_rows, weights, turned, width, strip)
+            state = (driver + symmetric_tiles(sums, other)) / denominator
+            continue
         regrouped = lax.all_to_all(rounded, "cd", split_axis=1, concat_axis=0, tiled=True)
         low = lax.all_gather(regrouped, "ab", axis=1, tiled=True)
         swapped_low = jnp.dot(all_swap, low, preferred_element_type=jnp.float32)

time: 392 us -> 328 us (0.84)
  Pallas kernels: 152 us -> 208 us
  blocking collectives: 36.8 us -> 0 us
  waiting for transfers between devices: 36.8 us -> 0 us
  local copies, waits for them, and re-layouts: 91.5 us -> 58.3 us
  other arithmetic: 33.1 us -> 54.1 us
  between operations: 13.9 us -> 0.68 us
  starting transfers between devices: 11 us -> 0 us
  matrix products: 15.5 us -> 6.61 us
    pallas_call x2, Pallas kernels: 152 us -> 208 us  [iteration_sums(): pl.pallas_call(functools.partial(iteration_kernel, bits, width, strip, ro...]
    all_to_all x2 -> x0, blocking collectives: 36.8 us -> none  [the longest x1 23.5 us: body(): lax.all_to_all(rounded, 'cd', split_axis=1, concat_axis=0, tiled=True)]
    all_gather x2 -> x0, waiting for transfers between devices: 33.7 us -> none  [body(): low = lax.all_gather(regrouped, 'ab', axis=1, tiled=True)]
    mul x2 -> x3, local copies, waits for them, and re-layouts: 0.25 us -> 25.4 us  [body(): weights * block_mask.astype(jnp.bfloat16)[:, None, :, None]]
    slice x11 -> x6, local copies, waits for them, and re-layouts: 23.6 us -> 3 us  [the longest x2 2.87 us: symmetric_tiles(): kept = sums[:, diag_cols:].reshape(rows_dev, 2, half, half)]
    convert_element_type x6 -> x0, local copies, waits for them, and re-layouts: 19.8 us -> none  [body(): symmetric = received + flip_tiles(tiles, tile_width).astype(jnp.float32)]
    dynamic_slice x2 -> x0, local copies, waits for them, and re-layouts: 18.9 us -> none  [the longest x1 11.3 us: body(): diag_tile = lax.dynamic_index_in_dim(weights, ab_index, 0, keepdims=False)]
    reshape x4 -> x12, local copies, waits for them, and re-layouts: 1.21 us -> 15.9 us  [the longest x4 5.5 us: symmetric_tiles(): came = swap_rows(other).reshape(rows_dev, 2, half, half).swapaxes(2, 3)]
  transfers between devices with their start and end apart: 4 -> 0, of which waited for: 3 -> 0; matrix products, arithmetic and copies ran while one was open for 21% -> 0% of each run, Pallas kernels for 0% -> 0%
where the time goes in v2:
time: 328 us
  Pallas kernels  208 us (63%)
  local copies, waits for them, and re-layouts  58.3 us (18%)
  other arithmetic  54.1 us (16%)
  matrix products  6.61 us (2%)
    pallas_call x2, Pallas kernels, iteration_sums(): pl.pallas_call(functools.partial(iteration_kernel, bits, width, strip, ro...  208 us
    mul x3, local copies, waits for them, and re-layouts, body(): weights * block_mask.astype(jnp.bfloat16)[:, None, :, None]  25.4 us
    mul x1, other arithmetic, body(): weights * block_mask.astype(jnp.bfloat16)[:, None, :, None]  15.8 us
    transpose x1, other arithmetic, body(): turned = jnp.swapaxes(weights, 1, 2)  11.3 us

profile of v2, /device:TPU:0, one launch (start us, length us, event | category | flops | bytes accessed | tf_op | source)
XLA Modules:
  0.0 327.6 jit_solution(9217398374316537478)
XLA Ops:
  0.0 2.4 convert_element_type.39.state_ref
  3.8 15.8 %copy_multiply_fusion = bf16[2,64,64,1024]{3,1,2,0:T(8,128)(2,1)S(1)} fusion(bf16[2,64,64,1024]{3,2,1,0:T(8,128)(2,1)} %bitcast.104, bf16[2,64,1024]{2,1,0:T(8,128)(2,1)S(1)} %mul.64), kind=kLoop, calls=%fused_computation | loop fusion | flops 8388608 | bytes 33816576 | tf_op jit(solution)/shard_map/mul | solution.py:502
  19.6 25.2 %copy.35.weight_ref = bf16[2,64,64,1024]{3,2,1,0:T(8,128)(2,1)} copy(bf16[2,64,64,1024]{3,1,2,0:T(8,128)(2,1)S(1)} %copy_multiply_fusion) | data formatting | bytes 33554432 | tf_op jit(solution)/shard_map/mul | solution.py:502
  44.8 11.3 %fusion.50.turned_ref = bf16[2,64,64,1024]{3,2,1,0:T(8,128)(2,1)} fusion(bf16[2,64,1024]{2,1,0:T(8,128)(2,1)S(1)} %mul.64, bf16[2,64,64,1024]{3,2,1,0:T(8,128)(2,1)S(1)} %bitcast.107), kind=kLoop, calls=%fused_computation.144 | loop fusion | flops 8388608 | bytes 33816576 | tf_op jit(solution)/shard_map/transpose | solution.py:510
  56.1 105.5 %shard_map.73 = (f32[48,4608]{1,0:T(8,128)}, bf16[48,2048]{1,0:T(8,128)(2,1)}) custom-call(bf16[48,8192]{1,0:T(8,128)(2,1)} %convert_element_type.39.state_ref, f32[768,128]{1,0:T(8,128)} %broadcast_in_dim.61.diagonal_ref, bf16[2,64,64,1024]{3,2,1,0:T(8,128)(2,1)} %copy.35.weight_ref, bf16[2,64,64,1024]{3,2,1,0:T(8,128)(2,1)} %fusion.50.turned_ref), custom_call_target="tpu_custom_call" | custom-call | tf_op jit(solution)/shard_map/pallas_call | solution.py:454
  165.9 1.7 fusion.9
  168.6 1.4 reshape.430
  176.8 1.4 reshape.426
  181.8 2.5 broadcast_select_fusion.3
  184.7 6.4 %fusion = f32[1,8192]{1,0:T(1,128)S(1)} fusion(s32[8192]{0:T(1024)S(1)} %get-tuple-element.55, s32[8192]{0:T(1024)S(1)} %get-tuple-element.54, f32[128]{0:T(128)S(1)} %copy-done), kind=kOutput, calls=%fused_computation.1 | convolution fusion | flops 17825792 | bytes 98816 | tf_op jit(solution)/shard_map/dot_general | solution.py:539
  192.9 102.4 %shard_map.74 = (f32[48,4608]{1,0:T(8,128)}, bf16[48,2048]{1,0:T(8,128)(2,1)}) custom-call(bf16[48,8192]{1,0:T(8,128)(2,1)} %fusion.6.state_ref, f32[768,128]{1,0:T(8,128)} %broadcast_in_dim.61.diagonal_ref, bf16[2,64,64,1024]{3,2,1,0:T(8,128)(2,1)} %copy.35.weight_ref, bf16[2,64,64,1024]{3,2,1,0:T(8,128)(2,1)} %fusion.50.turned_ref), custom_call_target="tpu_custom_call" | custom-call | tf_op jit(solution)/shard_map/pallas_call | solution.py:454
  295.3 1.8 slice.201
  297.1 1.5 reshape.436
  298.9 1.4 reshape.437
  300.4 2.3 copy.49
  302.7 1.6 fusion.10
  305.2 1.4 reshape.438
  314.2 1.4 reshape.434
  315.6 1.4 fusion.49
  317.1 1.4 fusion.48
  319.6 1.5 fusion.8
  321.2 1.9 copy.47
  324.4 1.8 broadcast_select_fusion.1
  326.2 1.4 subtract_divide_fusion
  (133 shorter events, 30.0 us)
Async XLA Ops:
  0.0 184.6 %copy-start = (f32[128]{0:T(128)S(1)}, f32[128]{0:T(128)}, u32[]{:S(2)}) copy-start(f32[128]{0:T(128)} %param.13) | copy-start | bytes 1540
  0.0 2.4 copy-start.22
  0.0 3.4 %copy-start.23 = (s32[64,8]{0,1:T(8,128)S(1)}, s32[64,8]{0,1:T(8,128)}, u32[]{:S(2)}) copy-start(s32[64,8]{0,1:T(8,128)} %param.10) | copy-start | bytes 6148
  3.7 41.1 %slice-start = ((s8[16777216]{0:T(1024)(128)(4,1)}), s8[4194304]{0:T(1024)(128)(4,1)S(1)}, s32[]{:S(2)}) async-start(s8[16777216]{0:T(1024)(128)(4,1)} %bitcast.105), calls=%async_computation | async-start | bytes 8388608
  3.8 41.1 %slice-start.1 = ((s8[16777216]{0:T(1024)(128)(4,1)}), s8[4194304]{0:T(1024)(128)(4,1)S(1)}, s32[]{:S(2)}) async-start(s8[16777216]{0:T(1024)(128)(4,1)} %bitcast.105), calls=%async_computation.1 | async-start | bytes 8388608
  3.8 41.0 %slice-start.2 = ((s8[16777216]{0:T(1024)(128)(4,1)}), s8[4194304]{0:T(1024)(128)(4,1)S(1)}, s32[]{:S(2)}) async-start(s8[16777216]{0:T(1024)(128)(4,1)} %bitcast.105), calls=%async_computation.2 | async-start | bytes 8388608
  19.6 25.2 %slice-start.3 = ((s8[16777216]{0:T(1024)(128)(4,1)}), s8[4194304]{0:T(1024)(128)(4,1)S(1)}, s32[]{:S(2)}) async-start(s8[16777216]{0:T(1024)(128)(4,1)} %bitcast.105), calls=%async_computation.3 | async-start | bytes 8388608
  161.7 1.6 copy-start.14
  175.1 1.7 copy-start.8
  178.4 1.1 copy-start.18
  180.3 1.4 copy-start.10
  180.3 1.4 copy-start.11
  181.7 2.5 copy-start.24
  181.7 2.5 copy-start.25
  181.7 2.5 copy-start.26
  184.6 7.1 %copy-start.1 = (f32[48,8192]{1,0:T(8,128)S(1)}, f32[48,8192]{1,0:T(8,128)}, u32[]{:S(2)}) copy-start(f32[48,8192]{1,0:T(8,128)} %param.8) | copy-start | bytes 4718596
  184.6 7.0 %copy-start.12 = (f32[48,4096]{1,0:T(8,128)S(1)}, f32[48,4096]{1,0:T(8,128)}, u32[]{:S(2)}) copy-start(f32[48,4096]{1,0:T(8,128)} %get-tuple-element.25) | copy-start | bytes 2359300
  184.6 7.0 %copy-start.13 = (f32[48,4096]{1,0:T(8,128)S(1)}, f32[48,4096]{1,0:T(8,128)}, u32[]{:S(2)}) copy-start(f32[48,4096]{1,0:T(8,128)} %get-tuple-element.26) | copy-start | bytes 2359300
  295.3 3.3 %copy-start.15 = (bf16[48,2048]{1,0:T(8,128)(2,1)S(1)}, bf16[48,2048]{1,0:T(8,128)(2,1)}, u32[]{:S(2)}) copy-start(bf16[48,2048]{1,0:T(8,128)(2,1)} %get-tuple-element.12) | copy-start | bytes 589828
  306.6 2.3 copy-start.19
  309.2 1.1 copy-start.6
  310.6 1.1 copy-start.4
  315.6 2.8 copy-start.3
  324.4 1.8 copy-start.21
  (7 other events, 6.4 us)

commit v3 on v2

--- a/solution.py
+++ b/solution.py
@@ -167,8 +167,8 @@
 
 
 def iteration_kernel(
-    bits, width, strip, rows, half,
-    state_ref, diagonal_ref, weight_ref, turned_ref, sums_ref, other_ref,
+    bits, width, rows,
+    state_ref, diagonal_ref, mask_ref, weight_ref, sums_ref, other_ref,
     low, straight, mirrored, outer, part, part_y, *rest,
 ):
     held = (part,) + rest[:bits]
@@ -180,10 +180,12 @@
     ab = lax.axis_index("ab")
     cd = lax.axis_index("cd")
     count = 1 << bits
-    tile_width = weight_ref.shape[1]
+    side = straight.shape[1]
+    strips = weight_ref.shape[1] // side
     depth = weight_ref.shape[3]
     piece = depth // 2
-    keeps = outer.shape[0] // (2 * width)
+    keeps = strips
+    span = width // (side * side)
     diags = keeps + 1
     products = 3 * keeps + 1
     finals = diags + keeps
@@ -197,35 +199,62 @@
             device_id=device, device_id_type=MESH,
         )
 
-    for s in range(tile_width // strip):
-        wide = tile_width - s * strip
-        base = sum(strip * (tile_width - r * strip) for r in range(s))
-
-        @pl.loop(0, strip)
-        def _(x):
-            rows_to = pl.ds(pl.multiple_of(base + x * wide, strip), wide)
-            rows_from = pl.ds(s * strip, wide)
-            pltpu.make_async_copy(
-                weight_ref.at[ab, s * strip + x, rows_from], straight.at[rows_to], load_sem.at[0]
-            ).start()
-            pltpu.make_async_copy(
-                turned_ref.at[ab, s * strip + x, rows_from], mirrored.at[rows_to], load_sem.at[1]
-            ).start()
-
-    @pl.loop(0, tile_width)
-    def _(x):
-        side = lax.rem(x // half + ab, 2)
-        kept = pl.ds(pl.multiple_of(side * half, half), half)
-        sent = pl.ds(pl.multiple_of((1 - side) * half, half), half)
-        to = pl.multiple_of(x * half, half)
+    def block_of(tile, x, y):
+        return weight_ref.at[
+            tile,
+            pl.ds(pl.multiple_of(x * side, side), side),
+            pl.ds(pl.multiple_of(y * side, side), side),
+        ]
+
+    def upper(p):
+        starts = [sum(strips - r for r in range(s)) for s in range(strips)]
+        x = sum((p >= start).astype(jnp.int32) for start in starts[1:])
+        start = sum(
+            jnp.where(x == s, starts[s], 0) for s in range(strips)
+        )
+        return x, p - start + x
+
+    def kept_y(p, which):
+        return span * lax.rem(p // (span * span) + which, 2) + lax.rem(p, span)
+
+    @pl.loop(0, diags * span)
+    def _(p):
+        x, y = upper(p)
+        pltpu.make_async_copy(block_of(ab, x, y), straight.at[p], load_sem.at[0]).start()
+        pltpu.make_async_copy(block_of(ab, y, x), mirrored.at[p], load_sem.at[1]).start()
+
+    @pl.loop(0, keeps * span)
+    def _(p):
         pltpu.make_async_copy(
-            weight_ref.at[1 - ab, x, kept], outer.at[pl.ds(to, half)], load_sem.at[2]
+            block_of(1 - ab, p // span, kept_y(p, ab)), outer.at[0, p], load_sem.at[2]
         ).start()
         pltpu.make_async_copy(
-            turned_ref.at[1 - ab, x, sent],
-            outer.at[pl.ds(to + tile_width * half, half)],
-            load_sem.at[2],
+            block_of(1 - ab, kept_y(p, 1 - ab), p // span), outer.at[1, p], load_sem.at[3]
         ).start()
+
+    def masked(block, tile, x):
+        pairs = side // 2
+        mask = mask_ref[tile, pl.ds(pl.multiple_of(x * pairs, pairs), pairs)]
+        value = block.reshape(pairs, 2, side, depth) * mask[:, None]
+        return value.reshape(side * side, depth)
+
+    area = side * side
+    row_at = lax.broadcasted_iota(jnp.int32, (area, area), 0)
+    col_at = lax.broadcasted_iota(jnp.int32, (area, area), 1)
+    turn_rows = (row_at == lax.rem(col_at, side) * side + col_at // side).astype(jnp.bfloat16)
+
+    def turned(value):
+        product = jnp.dot(turn_rows, value, preferred_element_type=jnp.float32)
+        return product.astype(jnp.bfloat16).reshape(side, side, depth)
+
+    def prepare_diag(p):
+        x, y = upper(p)
+        straight[p] = masked(straight[p], ab, x).reshape(side, side, depth)
+        mirrored[p] = turned(masked(mirrored[p], ab, y))
+
+    def prepare_outer(p):
+        outer[0, p] = masked(outer[0, p], 1 - ab, p // span).reshape(side, side, depth)
+        outer[1, p] = turned(masked(outer[1, p], 1 - ab, kept_y(p, 1 - ab)))
 
     barrier = pltpu.get_barrier_semaphore()
 
@@ -283,9 +312,25 @@
             scatter(cd, source).wait_recv()
             forward(source, ab).start()
 
-    pltpu.make_async_copy(straight, straight, load_sem.at[0]).wait()
-    pltpu.make_async_copy(mirrored, mirrored, load_sem.at[1]).wait()
-    pltpu.make_async_copy(outer, outer, load_sem.at[2]).wait()
+        @pl.when(i == 0)
+        def _():
+            pltpu.make_async_copy(straight, straight, load_sem.at[0]).wait()
+            pltpu.make_async_copy(mirrored, mirrored, load_sem.at[1]).wait()
+
+        @pl.when(i < diags * span)
+        def _():
+            prepare_diag(i)
+
+        late = i - (count - keeps * span)
+
+        @pl.when(late == 0)
+        def _():
+            pltpu.make_async_copy(outer.at[0], outer.at[0], load_sem.at[2]).wait()
+            pltpu.make_async_copy(outer.at[1], outer.at[1], load_sem.at[3]).wait()
+
+        @pl.when(late >= 0)
+        def _():
+            prepare_outer(late)
 
     @pl.loop(0, count)
     def _(i):
@@ -340,6 +385,9 @@
     def rows_at(start):
         return pl.ds(pl.multiple_of(start, width), width)
 
+    def blocks_at(turn):
+        return pl.ds(turn * span, span)
+
     def dot(left, right):
         return lax.dot_general(left, right, NT, preferred_element_type=jnp.float32)
 
@@ -354,14 +402,14 @@
 
         @pl.when(is_diag)
         def _():
-            total = dot(low[0], straight[rows_at(turn * width)])
-            put(step, total + dot(low[1], mirrored[rows_at(turn * width)]))
+            total = dot(low[0], straight[blocks_at(turn)].reshape(width, depth))
+            put(step, total + dot(low[1], mirrored[blocks_at(turn)].reshape(width, depth)))
             core_copy(step).start()
 
         @pl.when((kind != 1) & (step < 3 * keeps))
         def _():
             sent = 1 - kind // 2
-            put(step, dot(low[sent], outer[rows_at((sent * keeps + turn) * width)]))
+            put(step, dot(low[sent], outer[sent, blocks_at(turn)].reshape(width, depth)))
             core_copy(step).start()
 
         u = step - 1
@@ -438,33 +486,32 @@
             stage_copy(stage, q).wait_send()
 
 
-def iteration_sums(state, diagonal, weights, turned, width, strip):
+def iteration_sums(state, diagonal, mask, weights, width):
     rows = state.shape[0]
     count = diagonal.shape[0] // rows
     bits = count.bit_length() - 1
     tile_width, depth = weights.shape[1], weights.shape[3]
-    half = tile_width // 2
-    diag_cols = sum(
-        strip * (tile_width - s * strip) for s in range(tile_width // strip)
-    )
-    keeps = tile_width * half // width
+    keeps = tile_width // STRIP
+    diags = keeps + 1
+    span = width // (STRIP * STRIP)
     products, finals = 3 * keeps + 1, 2 * keeps + 1
     dma = pltpu.SemaphoreType.DMA
     block = (rows, width)
+    square = (STRIP, STRIP, depth)
     return pl.pallas_call(
-        functools.partial(iteration_kernel, bits, width, strip, rows, half),
+        functools.partial(iteration_kernel, bits, width, rows),
         out_shape=(
             jax.ShapeDtypeStruct((rows, finals * width), jnp.float32),
             jax.ShapeDtypeStruct((rows, keeps * width), jnp.bfloat16),
         ),
-        in_specs=[pl.BlockSpec(memory_space=pltpu.VMEM)] * 2
-        + [pl.BlockSpec(memory_space=pl.ANY)] * 2,
+        in_specs=[pl.BlockSpec(memory_space=pltpu.VMEM)] * 3
+        + [pl.BlockSpec(memory_space=pl.ANY)],
         out_specs=[pl.BlockSpec(memory_space=pltpu.VMEM)] * 2,
         scratch_shapes=[
             pltpu.VMEM((2, count * rows, depth), jnp.bfloat16),
-            pltpu.VMEM((diag_cols, depth), jnp.bfloat16),
-            pltpu.VMEM((diag_cols, depth), jnp.bfloat16),
-            pltpu.VMEM((2 * tile_width * half, depth), jnp.bfloat16),
+            pltpu.VMEM((diags * span,) + square, jnp.bfloat16),
+            pltpu.VMEM((diags * span,) + square, jnp.bfloat16),
+            pltpu.VMEM((2, keeps * span) + square, jnp.bfloat16),
             pltpu.VMEM((products,) + (2,) * bits + block, jnp.bfloat16),
             pltpu.VMEM((keeps,) + (2,) * (bits - 1) + block, jnp.bfloat16),
             pltpu.VMEM((products,) + (2,) * (bits - 1) + block, jnp.bfloat16),
@@ -474,7 +521,7 @@
             ],
             pltpu.VMEM((keeps,) + block, jnp.bfloat16),
             pltpu.VMEM((keeps,) + block, jnp.bfloat16),
-            dma((3,)), dma,
+            dma((4,)), dma,
             dma((count,)), dma((count,)), dma((count,)), dma((count,)),
             dma((products,)), dma((products,)), dma((keeps,)), dma((keeps,)),
             dma((bits - 1, finals)), dma((bits - 1, finals)), dma((keeps,)), dma((keeps,)),
@@ -482,7 +529,92 @@
         compiler_params=pltpu.CompilerParams(
             collective_id=1, has_side_effects=True, vmem_limit_bytes=60 * 2**20
         ),
-    )(state, diagonal, weights, turned)
+    )(state, diagonal, mask, weights)
+
+
+def update_kernel(
+    strips, side, span,
+    sums_ref, other_ref, driver_ref, cols_ref, rows_ref, same_ref, next_ref,
+):
+    ab = lax.axis_index("ab")
+    rows = driver_ref.shape[0]
+    area = side * side
+    wide = strips * area
+    tile_area = strips * wide
+    uppers = [(x, y) for x in range(strips) for y in range(x, strips)]
+
+    def iotas(size):
+        return (lax.broadcasted_iota(jnp.int32, (size, size), axis) for axis in (0, 1))
+
+    start, end = iotas(area)
+    turn = (start == lax.rem(end, side) * side + end // side).astype(jnp.bfloat16)
+    start, end = iotas(wide)
+    block, inner = lax.rem(end, strips * side) // side, lax.rem(end, side)
+    ordered = start == block * area + end // (strips * side) * side + inner
+    ordered = ordered.astype(jnp.bfloat16)
+    odd = lax.rem(lax.broadcasted_iota(jnp.int32, (rows, area), 0), 2) == 1
+    same = jnp.broadcast_to(same_ref[:, 0:1], (rows, area)) != 0
+
+    def swap(value):
+        return jnp.where(
+            same, value, jnp.where(odd, pltpu.roll(value, 1, 0), pltpu.roll(value, rows - 1, 0))
+        )
+
+    def sums_of(index):
+        return sums_ref[:, index * area : (index + 1) * area]
+
+    def exact_dot(value, right):
+        high = value.astype(jnp.bfloat16)
+        rest = (value - high.astype(jnp.float32)).astype(jnp.bfloat16)
+        return jnp.dot(high, right, preferred_element_type=jnp.float32) + jnp.dot(
+            rest, right, preferred_element_type=jnp.float32
+        )
+
+    lower = [swap(sums_of(p)) for p, (x, y) in enumerate(uppers) if x < y]
+    turned = exact_dot(jnp.concatenate(lower), turn)
+    diag, taken = {}, 0
+    for p, (x, y) in enumerate(uppers):
+        diag[x, y] = sums_of(p)
+        if x < y:
+            diag[y, x] = turned[taken * rows : (taken + 1) * rows]
+            taken += 1
+    came = [
+        swap(other_ref[:, p * area : (p + 1) * area].astype(jnp.float32))
+        for p in range(strips * span)
+    ]
+    came = jnp.dot(
+        jnp.concatenate(came).astype(jnp.bfloat16), turn, preferred_element_type=jnp.float32
+    )
+    even = ab == 0
+    off = {}
+    for x in range(strips):
+        for y in range(strips):
+            kept = sums_of(len(uppers) + x * span + y % span)
+            p = y * span + x % span
+            sent = came[p * rows : (p + 1) * rows]
+            if x // span == y // span:
+                off[x, y] = jnp.where(even, kept, sent)
+            else:
+                off[x, y] = jnp.where(even, sent, kept)
+    for tile, blocks in ((ab, diag), (1 - ab, off)):
+        for x in range(strips):
+            line = jnp.concatenate([blocks[x, y] for y in range(strips)], axis=1)
+            symmetric = exact_dot(line, ordered)
+            at = pl.ds(pl.multiple_of(tile * tile_area + x * wide, wide), wide)
+            below = cols_ref[:, at] - rows_ref[:, 0:1]
+            next_ref[:, at] = ((driver_ref[:, at] + symmetric) / below).astype(next_ref.dtype)
+
+
+def update(sums, other, driver, col_energy, row_energy, same, tile_width, width, dtype):
+    strips = tile_width // STRIP
+    span = width // (STRIP * STRIP)
+    return pl.pallas_call(
+        functools.partial(update_kernel, strips, STRIP, span),
+        out_shape=jax.ShapeDtypeStruct(driver.shape, dtype),
+        in_specs=[pl.BlockSpec(memory_space=pltpu.VMEM)] * 6,
+        out_specs=pl.BlockSpec(memory_space=pltpu.VMEM),
+        compiler_params=pltpu.CompilerParams(vmem_limit_bytes=48 * 2**20),
+    )(sums, other, driver, col_energy, row_energy, same)
 
 
 def body(amplitudes, driver, ladder, block_mask, pair_list, occ_energy, virt_energy):
@@ -498,16 +630,18 @@
     diag_cols = sum(strip * (tile_width - s * strip) for s in range(strips))
     width = min(512, tile_area)
 
+    paired = (
+        ab_count == 2
+        and tile_width % (2 * STRIP) == 0
+        and width == 2 * STRIP * STRIP
+        and diag_cols == (strips + 1) * width
+        and lax.axis_size("cd") >= 2 * (strips + 1)
+        and lax.axis_size("cd").bit_count() == 1
+    )
     weights = ladder.reshape(out_rows // BLK, BLK, in_cols // BLK, BLK)
     weights = (weights * block_mask.astype(jnp.bfloat16)[:, None, :, None]).reshape(
         ab_count, tile_width, tile_width, in_cols
     )
-    paired = (
-        ab_count == 2
-        and tile_area % (2 * width) == 0
-        and diag_cols == (tile_area // 2 // width + 1) * width
-    )
-    turned = jnp.swapaxes(weights, 1, 2)
     diag_tile = lax.dynamic_index_in_dim(weights, ab_index, 0, keepdims=False)
 
     def pack(tile):
@@ -565,47 +699,29 @@
 
     diag_rows = (pair_list // NOCC == pair_list % NOCC).astype(jnp.float32)
     diag_rows = jnp.broadcast_to(diag_rows[:, None], (pair_list.shape[0], 128))
-    odd_row = (jnp.arange(rows_dev) % 2 == 1)[:, None]
-    same_row = (row_pairs // NOCC == row_pairs % NOCC)[:, None]
-
-    def swap_rows(value):
-        above = jnp.concatenate([value[-1:], value[:-1]])
-        below = jnp.concatenate([value[1:], value[:1]])
-        return jnp.where(same_row, value, jnp.where(odd_row, above, below))
-
-    def symmetric_tiles(sums, other):
-        half = tile_width // 2
-        diag = spread(sums[:, :diag_cols])
-        diag = diag + flip_tiles(swap_rows(diag)[:, None, :], tile_width)
-        kept = sums[:, diag_cols:].reshape(rows_dev, 2, half, half)
-        came = swap_rows(other).reshape(rows_dev, 2, half, half).swapaxes(2, 3)
-        came = jnp.where(ab_index == 1, came, came[:, ::-1]).astype(jnp.float32)
-        first_half = jnp.concatenate(
-            [
-                jnp.where(ab_index == 0, kept[:, 0], came[:, 0]),
-                jnp.where(ab_index == 0, came[:, 0], kept[:, 0]),
-            ],
-            axis=2,
-        )
-        second_half = jnp.concatenate(
-            [
-                jnp.where(ab_index == 0, came[:, 1], kept[:, 1]),
-                jnp.where(ab_index == 0, kept[:, 1], came[:, 1]),
-            ],
-            axis=2,
-        )
-        off = jnp.concatenate([first_half, second_half], axis=1).reshape(rows_dev, tile_area)
-        return jnp.concatenate(
-            [jnp.where(ab_index == 0, diag, off), jnp.where(ab_index == 0, off, diag)], axis=1
-        )
+    row_same = (row_pairs // NOCC == row_pairs % NOCC).astype(jnp.float32)
+
+    def lanes(values):
+        return jnp.broadcast_to(values[:, None], (values.shape[0], 128))
+
+    if paired:
+        masks = block_mask.astype(jnp.bfloat16).reshape(ab_count, tile_area // BLK, 1, -1, 1)
+        masks = jnp.broadcast_to(
+            masks, (ab_count, tile_area // BLK, STRIP, in_cols // BLK, BLK)
+        ).reshape(ab_count, tile_area // BLK, STRIP, in_cols)
+        tiles_in = ladder.reshape(ab_count, tile_width, tile_width, in_cols)
+        state = amplitudes.astype(jnp.bfloat16)
+        for step in range(ITERS):
+            sums, other = iteration_sums(state, diag_rows, masks, tiles_in, width)
+            state = update(
+                sums, other, driver, col_energy[None, :], lanes(row_energy), lanes(row_same),
+                tile_width, width, jnp.bfloat16 if step < ITERS - 1 else jnp.float32,
+            )
+        return state
 
     state = amplitudes
     for step in range(ITERS):
         rounded = state.astype(jnp.bfloat16)
-        if paired:
-            sums, other = iteration_sums(rounded, diag_rows, weights, turned, width, strip)
-            state = (driver + symmetric_tiles(sums, other)) / denominator
-            continue
         regrouped = lax.all_to_all(rounded, "cd", split_axis=1, concat_axis=0, tiled=True)
         low = lax.all_gather(regrouped, "ab", axis=1, tiled=True)
         swapped_low = jnp.dot(all_swap, low, preferred_element_type=jnp.float32)

time: 328 us -> 237 us (0.72)
  other arithmetic: 54.1 us -> 3.36 us
  local copies, waits for them, and re-layouts: 58.3 us -> 8.02 us
  Pallas kernels: 208 us -> 218 us
    mul x7 -> x0, local copies, waits for them, and re-layouts: 26.1 us -> none  [the longest x3 25.4 us: body(): weights * block_mask.astype(jnp.bfloat16)[:, None, :, None]]
    mul x9 -> x0, other arithmetic: 18 us -> none  [the longest x1 15.8 us: body(): weights * block_mask.astype(jnp.bfloat16)[:, None, :, None]]
    reshape x18 -> x0, local copies, waits for them, and re-layouts: 16.8 us -> none  [the longest x4 5.5 us: symmetric_tiles(): came = swap_rows(other).reshape(rows_dev, 2, half, half).swapaxes(2, 3)]
    transpose x3 -> x0, other arithmetic: 13.2 us -> none  [the longest x1 11.3 us: body(): turned = jnp.swapaxes(weights, 1, 2)]
    pallas_call x2 -> x4, Pallas kernels: 208 us -> 218 us  [the longest x2 206 us: iteration_sums(): pl.pallas_call(functools.partial(iteration_kernel, bits, width, rows), ou...]
    concatenate x11 -> x0, other arithmetic: 8.28 us -> none  [the longest x6 4.79 us: spread(): return jnp.concatenate(pieces, axis=1).reshape(rows_dev, tile_area)]
    slice x16 -> x0, local copies, waits for them, and re-layouts: 6.57 us -> none  [the longest x6 2.94 us: spread(): piece = packed[:, start:start + strip * wide].reshape(rows_dev, strip, wide)]
    select_n x7 -> x0, other arithmetic: 5.54 us -> none  [the longest x2 4.27 us: symmetric_tiles(): jnp.where(ab_index == 0, diag, off)]
where the time goes in v3:
time: 237 us; the launch traced here: 236 us
  Pallas kernels  218 us (92%)
  local copies, waits for them, and re-layouts  8.02 us (3%)
  matrix products  7.26 us (3%)
  other arithmetic  3.36 us (1%)
    pallas_call x2, Pallas kernels, iteration_sums(): pl.pallas_call(functools.partial(iteration_kernel, bits, width, rows), ou...  206 us
    pallas_call x2, Pallas kernels, update(): pl.pallas_call(functools.partial(update_kernel, strips, STRIP, span), out...  11.4 us
    dot_general x1, matrix products, body(): col_energy = jnp.dot(picks, virt_energy, precision=lax.Precision.HIGHEST)  6.41 us
    unnamed x16, local copies, waits for them, and re-layouts  5.06 us

profile of v3, /device:TPU:0, one launch (start us, length us, event | category | flops | bytes accessed | tf_op | source)
XLA Modules:
  0.0 236.5 jit_solution(8044495226095122959)
XLA Ops:
  0.0 0.9 compare_convert_fusion
  0.9 0.9 convolution_bitcast_fusion
  1.7 0.7 convert_element_type.26
  2.5 0.7 fusion.30
  3.2 0.1 copy.9
  3.3 0.1 broadcast_in_dim.22.rows_ref
  3.3 0.1 broadcast_in_dim.23.same_ref
  3.4 0.1 fusion.8
  3.5 6.4 %fusion.cols_ref = f32[1,8192]{1,0:T(1,128)S(1)} fusion(s32[8192]{0:T(1024)S(1)} %get-tuple-element.17, s32[8192]{0:T(1024)S(1)} %get-tuple-element.16, f32[128]{0:T(128)S(1)} %copy-done), kind=kOutput, calls=%fused_computation | convolution fusion | flops 17825792 | bytes 98816 | tf_op jit(solution)/shard_map/dot_general | solution.py:673
  9.9 0.1 broadcast_in_dim.18
  10.1 0.1 broadcast_in_dim.19
  10.1 0.9 broadcast_in_dim.16.diagonal_ref
  11.1 1.0 convert_element_type.24.state_ref
  12.0 1.6 broadcast_in_dim.20.mask_ref
  13.6 104.7 %shard_map.73 = (f32[48,4608]{1,0:T(8,128)}, bf16[48,2048]{1,0:T(8,128)(2,1)}) custom-call(bf16[48,8192]{1,0:T(8,128)(2,1)} %convert_element_type.24.state_ref, f32[768,128]{1,0:T(8,128)} %broadcast_in_dim.16.diagonal_ref, bf16[2,32,16,1024]{3,2,1,0:T(8,128)(2,1)} %broadcast_in_dim.20.mask_ref, bf16[2,64,64,1024]{3,2,1,0:T(8,128)(2,1)} %bitcast.13), custom_call_target="tpu_custom_call" | custom-call | tf_op jit(solution)/shard_map/pallas_call | solution.py:501
  118.4 1.2 copy-done.4
  119.5 0.9 copy-done.6
  120.5 5.1 %shard_map.74.state_ref = bf16[48,8192]{1,0:T(8,128)(2,1)S(1)} custom-call(f32[48,4608]{1,0:T(8,128)S(1)} %copy-done.4, bf16[48,2048]{1,0:T(8,128)(2,1)S(1)} %copy-done.6, f32[48,8192]{1,0:T(8,128)S(1)} %copy-done.1, f32[1,8192]{1,0:T(1,128)S(1)} %fusion.cols_ref, f32[48,128]{1,0:T(8,128)S(1)} %broadcast_in_dim.22.rows_ref, ...), custom_call_target="tpu_custom_call" | custom-call | tf_op jit(solution)/shard_map/pallas_call | solution.py:611
  125.6 0.0 copy-start.2
  125.6 0.9 copy-done.2
  126.5 101.6 %shard_map.75 = (f32[48,4608]{1,0:T(8,128)}, bf16[48,2048]{1,0:T(8,128)(2,1)}) custom-call(bf16[48,8192]{1,0:T(8,128)(2,1)} %copy-done.2, f32[768,128]{1,0:T(8,128)} %broadcast_in_dim.16.diagonal_ref, bf16[2,32,16,1024]{3,2,1,0:T(8,128)(2,1)} %broadcast_in_dim.20.mask_ref, bf16[2,64,64,1024]{3,2,1,0:T(8,128)(2,1)} %bitcast.14), custom_call_target="tpu_custom_call" | custom-call | tf_op jit(solution)/shard_map/pallas_call | solution.py:501
  228.1 1.2 copy-done.3
  229.3 0.9 copy-done.5
  230.2 6.3 %shard_map.76 = f32[48,8192]{1,0:T(8,128)} custom-call(f32[48,4608]{1,0:T(8,128)S(1)} %copy-done.3, bf16[48,2048]{1,0:T(8,128)(2,1)S(1)} %copy-done.5, f32[48,8192]{1,0:T(8,128)S(1)} %copy-done.1, f32[1,8192]{1,0:T(1,128)S(1)} %fusion.cols_ref, f32[48,128]{1,0:T(8,128)S(1)} %broadcast_in_dim.22.rows_ref, f32[48,128]{1,0:T(8,128)S(1)} %broadcast_in_dim.23.same_ref), custom_call_target="tpu_custom_call" | custom-call | tf_op jit(solution)/shard_map/pallas_call | solution.py:611
  (10 shorter events, 0.0 us)
Async XLA Ops:
  0.0 3.5 %copy-start = (f32[128]{0:T(128)S(1)}, f32[128]{0:T(128)}, u32[]{:S(2)}) copy-start(f32[128]{0:T(128)} %param.13) | copy-start | bytes 1540
  0.0 11.1 %copy-start.7 = (f32[48,8192]{1,0:T(8,128)S(1)}, f32[48,8192]{1,0:T(8,128)}, u32[]{:S(2)}) copy-start(f32[48,8192]{1,0:T(8,128)} %param.7) | copy-start | bytes 4718596
  13.6 104.7 %copy-start.1 = (f32[48,8192]{1,0:T(8,128)S(1)}, f32[48,8192]{1,0:T(8,128)}, u32[]{:S(2)}) copy-start(f32[48,8192]{1,0:T(8,128)} %driver_ref.3) | copy-start | bytes 4718596
  118.4 1.2 copy-start.4
  119.5 0.9 copy-start.6
  125.6 0.9 copy-start.2
  228.1 1.2 copy-start.3
  229.3 0.9 copy-start.5

commit v4 on v3

--- a/solution.py
+++ b/solution.py
@@ -291,52 +291,49 @@
     )
     stay.start()
 
+    def other(j):
+        return sum(
+            lax.rem(own[bit] + bit_of(j, bit), 2) * (1 << bit) for bit in range(bits)
+        )
+
+    @pl.loop(1, count)
+    def _(i):
+        scatter(other(i), cd).start()
+
+    stay.wait()
+    forward(cd, ab).start()
+
     @pl.loop(0, count)
     def _(i):
-        j = lax.rem(i + count // 2, count)
-
-        @pl.when(j != 0)
-        def _():
-            scatter(lax.rem(cd + j, count), cd).start()
-
-    stay.wait()
-    forward(cd, ab).start()
+        @pl.when(i != 0)
+        def _():
+            source = other(i)
+            scatter(cd, source).wait_recv()
+            forward(source, ab).start()
+
+        @pl.when(i == 0)
+        def _():
+            pltpu.make_async_copy(straight, straight, load_sem.at[0]).wait()
+            pltpu.make_async_copy(mirrored, mirrored, load_sem.at[1]).wait()
+
+        @pl.when(i < diags * span)
+        def _():
+            prepare_diag(i)
+
+        late = i - (count - keeps * span)
+
+        @pl.when(late == 0)
+        def _():
+            pltpu.make_async_copy(outer.at[0], outer.at[0], load_sem.at[2]).wait()
+            pltpu.make_async_copy(outer.at[1], outer.at[1], load_sem.at[3]).wait()
+
+        @pl.when(late >= 0)
+        def _():
+            prepare_outer(late)
 
     @pl.loop(0, count)
     def _(i):
-        j = lax.rem(i + count // 2, count)
-
-        @pl.when(j != 0)
-        def _():
-            source = lax.rem(cd + count - j, count)
-            scatter(cd, source).wait_recv()
-            forward(source, ab).start()
-
-        @pl.when(i == 0)
-        def _():
-            pltpu.make_async_copy(straight, straight, load_sem.at[0]).wait()
-            pltpu.make_async_copy(mirrored, mirrored, load_sem.at[1]).wait()
-
-        @pl.when(i < diags * span)
-        def _():
-            prepare_diag(i)
-
-        late = i - (count - keeps * span)
-
-        @pl.when(late == 0)
-        def _():
-            pltpu.make_async_copy(outer.at[0], outer.at[0], load_sem.at[2]).wait()
-            pltpu.make_async_copy(outer.at[1], outer.at[1], load_sem.at[3]).wait()
-
-        @pl.when(late >= 0)
-        def _():
-            prepare_outer(late)
-
-    @pl.loop(0, count)
-    def _(i):
-        j = lax.rem(i + count // 2, count)
-        source = lax.rem(cd + count - j, count)
-        forward(source, 1 - ab).wait_recv()
+        forward(other(i), 1 - ab).wait_recv()
 
     odd = lax.rem(lax.broadcasted_iota(jnp.int32, (rows, 128), 0), 2) == 1
 
@@ -710,11 +707,15 @@
             masks, (ab_count, tile_area // BLK, STRIP, in_cols // BLK, BLK)
         ).reshape(ab_count, tile_area // BLK, STRIP, in_cols)
         tiles_in = ladder.reshape(ab_count, tile_width, tile_width, in_cols)
+        first_energy = lax.dynamic_slice_in_dim(virt_energy, ab_index * tile_width, tile_width)
+        tile_energy = (
+            first_energy[None, :, None] + virt_energy.reshape(ab_count, 1, tile_width)
+        ).reshape(1, cols_dev)
         state = amplitudes.astype(jnp.bfloat16)
         for step in range(ITERS):
             sums, other = iteration_sums(state, diag_rows, masks, tiles_in, width)
             state = update(
-                sums, other, driver, col_energy[None, :], lanes(row_energy), lanes(row_same),
+                sums, other, driver, tile_energy, lanes(row_energy), lanes(row_same),
                 tile_width, width, jnp.bfloat16 if step < ITERS - 1 else jnp.float32,
             )
         return state

time: 237 us -> 219 us (0.924)
  Pallas kernels: 218 us -> 204 us
  matrix products: 7.26 us -> 0.2 us
    pallas_call x2, Pallas kernels: 206 us -> 193 us  [iteration_sums(): pl.pallas_call(functools.partial(iteration_kernel, bits, width, rows), ou...]
    dot_general x1 -> x0, matrix products: 6.41 us -> none  [body(): col_energy = jnp.dot(picks, virt_energy, precision=lax.Precision.HIGHEST)]
    unnamed x16 -> x14, local copies, waits for them, and re-layouts: 5.06 us -> 5.06 us
where the time goes in v4:
time: 219 us; the launch traced here: 218 us
  Pallas kernels  204 us (93%)
  local copies, waits for them, and re-layouts  9.59 us (4%)
  other arithmetic  4.62 us (2%)
    pallas_call x2, Pallas kernels, iteration_sums(): pl.pallas_call(functools.partial(iteration_kernel, bits, width, rows), ou...  193 us
    pallas_call x2, Pallas kernels, update(): pl.pallas_call(functools.partial(update_kernel, strips, STRIP, span), out...  11.4 us
    unnamed x14, local copies, waits for them, and re-layouts  5.06 us

profile of v4, /device:TPU:0, one launch (start us, length us, event | category | flops | bytes accessed | tf_op | source)
XLA Modules:
  0.0 218.4 jit_solution(13233986931911360865)
XLA Ops:
  0.0 0.7 dynamic_slice.6
  0.7 0.7 add.58
  1.5 0.8 compare_convert_fusion
  2.3 0.2 convolution_bitcast_fusion
  2.5 0.7 convert_element_type.20
  3.2 0.7 fusion.10
  3.9 0.1 copy.9
  4.0 0.1 broadcast_in_dim.19.rows_ref
  4.0 0.1 broadcast_in_dim.20.same_ref
  4.1 0.1 broadcast_add_fusion
  4.2 0.1 add.61.cols_ref
  4.3 0.1 broadcast_in_dim.16
  4.5 0.9 broadcast_in_dim.14.diagonal_ref
  5.4 2.4 %convert_element_type.18.state_ref = bf16[48,8192]{1,0:T(8,128)(2,1)} convert(f32[48,8192]{1,0:T(8,128)} %param.7) | non-fusion elementwise | flops 393216 | bytes 2359296 | tf_op jit(solution)/shard_map/convert_element_type | solution.py:714
  7.8 1.6 broadcast_in_dim.18.mask_ref
  9.4 98.5 %shard_map.73 = (f32[48,4608]{1,0:T(8,128)}, bf16[48,2048]{1,0:T(8,128)(2,1)}) custom-call(bf16[48,8192]{1,0:T(8,128)(2,1)} %convert_element_type.18.state_ref, f32[768,128]{1,0:T(8,128)} %broadcast_in_dim.14.diagonal_ref, bf16[2,32,16,1024]{3,2,1,0:T(8,128)(2,1)} %broadcast_in_dim.18.mask_ref, bf16[2,64,64,1024]{3,2,1,0:T(8,128)(2,1)} %bitcast.9), custom_call_target="tpu_custom_call" | custom-call | tf_op jit(solution)/shard_map/pallas_call | solution.py:498
  107.9 1.2 copy-done.4
  109.1 0.9 copy-done.6
  110.0 5.1 %shard_map.74.state_ref = bf16[48,8192]{1,0:T(8,128)(2,1)S(1)} custom-call(f32[48,4608]{1,0:T(8,128)S(1)} %copy-done.4, bf16[48,2048]{1,0:T(8,128)(2,1)S(1)} %copy-done.6, f32[48,8192]{1,0:T(8,128)S(1)} %copy-done.1, f32[1,8192]{1,0:T(1,128)S(1)} %add.61.cols_ref, f32[48,128]{1,0:T(8,128)S(1)} %broadcast_in_dim.19.rows_ref, ...), custom_call_target="tpu_custom_call" | custom-call | tf_op jit(solution)/shard_map/pallas_call | solution.py:608
  115.1 0.9 copy-done.2
  116.0 94.0 %shard_map.75 = (f32[48,4608]{1,0:T(8,128)}, bf16[48,2048]{1,0:T(8,128)(2,1)}) custom-call(bf16[48,8192]{1,0:T(8,128)(2,1)} %copy-done.2, f32[768,128]{1,0:T(8,128)} %broadcast_in_dim.14.diagonal_ref, bf16[2,32,16,1024]{3,2,1,0:T(8,128)(2,1)} %broadcast_in_dim.18.mask_ref, bf16[2,64,64,1024]{3,2,1,0:T(8,128)(2,1)} %bitcast.10), custom_call_target="tpu_custom_call" | custom-call | tf_op jit(solution)/shard_map/pallas_call | solution.py:498
  210.0 1.2 copy-done.3
  211.2 0.9 copy-done.5
  212.1 6.3 %shard_map.76 = f32[48,8192]{1,0:T(8,128)} custom-call(f32[48,4608]{1,0:T(8,128)S(1)} %copy-done.3, bf16[48,2048]{1,0:T(8,128)(2,1)S(1)} %copy-done.5, f32[48,8192]{1,0:T(8,128)S(1)} %copy-done.1, f32[1,8192]{1,0:T(1,128)S(1)} %add.61.cols_ref, f32[48,128]{1,0:T(8,128)S(1)} %broadcast_in_dim.19.rows_ref, f32[48,128]{1,0:T(8,128)S(1)} %broadcast_in_dim.20.same_ref), custom_call_target="tpu_custom_call" | custom-call | tf_op jit(solution)/shard_map/pallas_call | solution.py:608
  (10 shorter events, 0.1 us)
Async XLA Ops:
  0.0 2.2 %copy-start = (f32[32]{0:T(128)S(1)}, f32[32]{0:T(128)}, u32[]{:S(2)}) copy-start(f32[32]{0:T(128)} %param.12) | copy-start | bytes 388
  9.4 98.5 %copy-start.1 = (f32[48,8192]{1,0:T(8,128)S(1)}, f32[48,8192]{1,0:T(8,128)}, u32[]{:S(2)}) copy-start(f32[48,8192]{1,0:T(8,128)} %driver_ref.3) | copy-start | bytes 4718596
  107.9 1.2 copy-start.4
  109.1 0.9 copy-start.6
  115.1 0.9 copy-start.2
  210.0 1.2 copy-start.3
  211.2 0.9 copy-start.5

commit v5 on v4

--- a/solution.py
+++ b/solution.py
@@ -12,6 +12,7 @@
 BLK = 128
 ITERS = 2
 STRIP = 16
+GROUP = 16
 MESH = pl.DeviceIdType.MESH
 NT = (((1,), (1,)), ((), ()))
 
@@ -167,7 +168,7 @@
 
 
 def iteration_kernel(
-    bits, width, rows,
+    bits, width, rows, groups,
     state_ref, diagonal_ref, mask_ref, weight_ref, sums_ref, other_ref,
     low, straight, mirrored, outer, part, part_y, *rest,
 ):
@@ -273,43 +274,66 @@
     def cols_of(side):
         return pl.ds(pl.multiple_of(side * piece, piece), piece)
 
-    def scatter(target, source):
+    def scatter(group, target, source):
         return remote(
-            state_ref.at[:, pl.ds(pl.multiple_of(target * piece, piece), piece)],
-            low.at[0, rows_of(source), cols_of(ab)],
-            a_send.at[target], a_recv.at[source], (ab, target),
-        )
-
-    def forward(source, side):
-        block = low.at[0, rows_of(source), cols_of(side)]
-        return remote(block, block, b_send.at[source], b_recv.at[source], across)
-
-    stay = pltpu.make_async_copy(
-        state_ref.at[:, pl.ds(pl.multiple_of(cd * piece, piece), piece)],
-        low.at[0, rows_of(cd), cols_of(ab)],
-        self_sem,
-    )
-    stay.start()
+            state_ref.at[rows_of(group), cols_of(target)],
+            low.at[0, group, rows_of(source), cols_of(ab)],
+            a_send.at[group, target], a_recv.at[group, source], (ab, target),
+        )
+
+    def stay(group):
+        return pltpu.make_async_copy(
+            state_ref.at[rows_of(group), cols_of(cd)],
+            low.at[0, group, rows_of(cd), cols_of(ab)],
+            self_sem.at[group],
+        )
+
+    def forward(group, source, side):
+        block = low.at[0, group, rows_of(source), cols_of(side)]
+        return remote(block, block, b_send.at[group, source], b_recv.at[group, source], across)
 
     def other(j):
         return sum(
             lax.rem(own[bit] + bit_of(j, bit), 2) * (1 << bit) for bit in range(bits)
         )
 
-    @pl.loop(1, count)
-    def _(i):
-        scatter(other(i), cd).start()
-
-    stay.wait()
-    forward(cd, ab).start()
+    odd = lax.rem(lax.broadcasted_iota(jnp.int32, (rows, 128), 0), 2) == 1
+
+    def pass_on(group, i):
+        @pl.when(i == 0)
+        def _():
+            stay(group).wait()
+            forward(group, cd, ab).start()
+
+        @pl.when(i != 0)
+        def _():
+            source = other(i)
+            scatter(group, cd, source).wait_recv()
+            forward(group, source, ab).start()
+
+    def take_in(group, i):
+        source = other(i)
+        forward(group, source, 1 - ab).wait_recv()
+        at = rows_of(source)
+        same = diagonal_ref[group, at, :] != 0
+        for lane in range(0, depth, 128):
+            value = low[0, group, at, lane : lane + 128].astype(jnp.float32)
+            mate = jnp.where(odd, pltpu.roll(value, 1, 0), pltpu.roll(value, rows - 1, 0))
+            value = jnp.where(same, value, mate)
+            low[1, group, at, lane : lane + 128] = value.astype(jnp.bfloat16)
+
+    def send_group(group):
+        stay(group).start()
+
+        @pl.loop(1, count)
+        def _(i):
+            scatter(group, other(i), cd).start()
+
+    send_group(0)
 
     @pl.loop(0, count)
     def _(i):
-        @pl.when(i != 0)
-        def _():
-            source = other(i)
-            scatter(cd, source).wait_recv()
-            forward(source, ab).start()
+        pass_on(0, i)
 
         @pl.when(i == 0)
         def _():
@@ -331,29 +355,22 @@
         def _():
             prepare_outer(late)
 
+    if groups > 1:
+        send_group(1)
+
     @pl.loop(0, count)
     def _(i):
-        forward(other(i), 1 - ab).wait_recv()
-
-    odd = lax.rem(lax.broadcasted_iota(jnp.int32, (rows, 128), 0), 2) == 1
-
-    @pl.loop(0, count)
-    def _(source):
-        at = rows_of(source)
-        same = diagonal_ref[at, :] != 0
-        for lane in range(0, depth, 128):
-            value = low[0, at, lane : lane + 128].astype(jnp.float32)
-            other = jnp.where(odd, pltpu.roll(value, 1, 0), pltpu.roll(value, rows - 1, 0))
-            low[1, at, lane : lane + 128] = jnp.where(same, value, other).astype(jnp.bfloat16)
+        take_in(0, i)
 
     def at(stage, index, which):
         lead = (slice(None),) * (bits - 1 - stage)
         return held[stage].at[(index,) + lead + (which,)]
 
     def place(q):
-        turn = q // 2
+        inside = lax.rem(q, finals)
+        turn = inside // 2
         diag = jnp.where(turn == keeps, 3 * keeps, 3 * turn + 1)
-        return jnp.where(lax.rem(q, 2) == 0, diag, 3 * turn + 2)
+        return q // finals * products + jnp.where(lax.rem(inside, 2) == 0, diag, 3 * turn + 2)
 
     def core_copy(u):
         return remote(
@@ -361,7 +378,8 @@
         )
 
     def y_copy(j):
-        return remote(held[1].at[3 * j], part_y.at[j], y_send.at[j], y_recv.at[j], across)
+        sent = j // keeps * products + 3 * lax.rem(j, keeps)
+        return remote(held[1].at[sent], part_y.at[j], y_send.at[j], y_recv.at[j], across)
 
     def stage_copy(stage, q):
         source = at(1, place(q), 1 - own[1]) if stage == 1 else at(stage, q, 1 - own[stage])
@@ -388,56 +406,82 @@
     def dot(left, right):
         return lax.dot_general(left, right, NT, preferred_element_type=jnp.float32)
 
-    y_lag = 7
-    lags = [5 + 2 * s for s in range(bits - 1)]
-
-    @pl.loop(0, 2 * (finals - 1) + lags[-1] + 1)
+    y_lag = 8
+    lags = [11 + 3 * stage for stage in range(bits - 1)]
+    sources = count // 8
+
+    @pl.loop(0, (products * (groups * finals - 1)) // finals + lags[-1] + 1)
     def _(step):
-        turn = step // 3
-        kind = lax.rem(step, 3)
-        is_diag = ((kind == 1) & (step < 3 * keeps)) | (step == 3 * keeps)
-
-        @pl.when(is_diag)
-        def _():
-            total = dot(low[0], straight[blocks_at(turn)].reshape(width, depth))
-            put(step, total + dot(low[1], mirrored[blocks_at(turn)].reshape(width, depth)))
+        group = step // products
+        turn = lax.rem(step, products) // 3
+        kind = lax.rem(lax.rem(step, products), 3)
+        last = lax.rem(step, products) == 3 * keeps
+
+        @pl.when((group < groups) & ((kind == 1) | last))
+        def _():
+            total = dot(low[0, group], straight[blocks_at(turn)].reshape(width, depth))
+            total += dot(low[1, group], mirrored[blocks_at(turn)].reshape(width, depth))
+            put(step, total)
             core_copy(step).start()
 
-        @pl.when((kind != 1) & (step < 3 * keeps))
+        @pl.when((group < groups) & (kind != 1) & ~last)
         def _():
             sent = 1 - kind // 2
-            put(step, dot(low[sent], outer[sent, blocks_at(turn)].reshape(width, depth)))
+            right = outer[sent, blocks_at(turn)].reshape(width, depth)
+            put(step, dot(low[sent, group], right))
             core_copy(step).start()
 
         u = step - 1
 
-        @pl.when((u >= 0) & (u < products))
+        @pl.when((u >= 0) & (u < groups * products))
         def _():
             core_copy(u).wait_recv()
             held[1][u] = held[1][u] + at(0, u, own[0])[...]
-            u_kind = lax.rem(u, 3)
-
-            @pl.when((u_kind == 1) | (u == 3 * keeps))
+            u_group = u // products
+            u_step = lax.rem(u, products)
+            u_kind = lax.rem(u_step, 3)
+
+            @pl.when((u_kind == 1) | (u_step == 3 * keeps))
             def _():
-                stage_copy(1, 2 * (u // 3)).start()
-
-            @pl.when((u_kind == 0) & (u < 3 * keeps))
+                stage_copy(1, u_group * finals + 2 * (u_step // 3)).start()
+
+            @pl.when((u_kind == 0) & (u_step < 3 * keeps))
             def _():
-                y_copy(u // 3).start()
+                y_copy(u_group * keeps + u_step // 3).start()
+
+        arriving = lax.rem(step, products)
+
+        @pl.when((group + 2 < groups) & (arriving == 9))
+        def _():
+            send_group(group + 2)
+
+        @pl.when((group + 1 < groups) & (arriving >= 0) & (arriving < 8))
+        def _():
+            for i in range(sources):
+                pass_on(group + 1, (arriving - 0) * sources + i)
+
+        @pl.when((group + 1 < groups) & (arriving >= 9) & (arriving < 13))
+        def _():
+            for i in range(2 * sources):
+                take_in(group + 1, (arriving - 9) * 2 * sources + i)
 
         v = step - y_lag
-
-        @pl.when((v >= 0) & (lax.rem(v + 3, 3) == 0) & (v < 3 * keeps))
-        def _():
-            y_copy(v // 3).wait_recv()
-            held[1][v + 2] = held[1][v + 2] + part_y[v // 3]
-            stage_copy(1, 2 * (v // 3) + 1).start()
+        v_step = lax.rem(v + products, products)
+
+        @pl.when(
+            (v >= 0) & (v < groups * products) & (lax.rem(v_step, 3) == 0) & (v_step < 3 * keeps)
+        )
+        def _():
+            j = v_step // 3
+            y_copy(v // products * keeps + j).wait_recv()
+            held[1][v + 2] = held[1][v + 2] + part_y[v // products * keeps + j]
+            stage_copy(1, v // products * finals + 2 * j + 1).start()
 
         for stage in range(1, bits):
             w = step - lags[stage - 1]
-            q = w // 2
-
-            @pl.when((w >= 0) & (lax.rem(w + 2, 2) == 0) & (q < finals))
+            q = (finals * w + products - 1) // products
+
+            @pl.when((w >= 0) & ((products * q) // finals == w) & (q < groups * finals))
             def _():
                 stage_copy(stage, q).wait_recv()
                 index = place(q) if stage == 1 else q
@@ -447,37 +491,43 @@
                     stage_copy(stage + 1, q).start()
                 else:
                     total = held[stage + 1][q].astype(jnp.float32) + mine.astype(jnp.float32)
-                    kept = lax.rem(q, 2) == 1
-                    start = jnp.where(kept, diags + q // 2, q // 2) * width
-                    sums_ref[:, rows_at(start)] = total
+                    inside = lax.rem(q, finals)
+                    kept = lax.rem(inside, 2) == 1
+                    start = jnp.where(kept, diags + inside // 2, inside // 2) * width
+                    sums_ref[rows_of(q // finals), rows_at(start)] = total
 
                     @pl.when(kept)
                     def _():
-                        final[q // 2] = total.astype(jnp.bfloat16)
-                        last_copy(q // 2).start()
-
-    for j in range(keeps):
-        last_copy(j).wait_recv()
-        other_ref[:, j * width : (j + 1) * width] = landed[j]
-
-    @pl.loop(0, count)
-    def _(i):
-        @pl.when(i != cd)
-        def _():
-            scatter(i, cd).wait_send()
-
-        forward(i, ab).wait_send()
-
-    @pl.loop(0, products)
+                        j = q // finals * keeps + inside // 2
+                        final[j] = total.astype(jnp.bfloat16)
+                        last_copy(j).start()
+
+    @pl.loop(0, groups)
+    def _(group):
+        for j in range(keeps):
+            last_copy(group * keeps + j).wait_recv()
+            other_ref[rows_of(group), j * width : (j + 1) * width] = landed[group * keeps + j]
+
+    @pl.loop(0, groups)
+    def _(group):
+        @pl.loop(0, count)
+        def _(i):
+            @pl.when(i != cd)
+            def _():
+                scatter(group, i, cd).wait_send()
+
+            forward(group, i, ab).wait_send()
+
+    @pl.loop(0, groups * products)
     def _(u):
         core_copy(u).wait_send()
 
-    @pl.loop(0, keeps)
+    @pl.loop(0, groups * keeps)
     def _(j):
         y_copy(j).wait_send()
         last_copy(j).wait_send()
 
-    @pl.loop(0, finals)
+    @pl.loop(0, groups * finals)
     def _(q):
         for stage in range(1, bits):
             stage_copy(stage, q).wait_send()
@@ -485,7 +535,8 @@
 
 def iteration_sums(state, diagonal, mask, weights, width):
     rows = state.shape[0]
-    count = diagonal.shape[0] // rows
+    groups = rows // GROUP
+    count = diagonal.shape[1] // GROUP
     bits = count.bit_length() - 1
     tile_width, depth = weights.shape[1], weights.shape[3]
     keeps = tile_width // STRIP
@@ -493,10 +544,10 @@
     span = width // (STRIP * STRIP)
     products, finals = 3 * keeps + 1, 2 * keeps + 1
     dma = pltpu.SemaphoreType.DMA
-    block = (rows, width)
+    block = (GROUP, width)
     square = (STRIP, STRIP, depth)
     return pl.pallas_call(
-        functools.partial(iteration_kernel, bits, width, rows),
+        functools.partial(iteration_kernel, bits, width, GROUP, groups),
         out_shape=(
             jax.ShapeDtypeStruct((rows, finals * width), jnp.float32),
             jax.ShapeDtypeStruct((rows, keeps * width), jnp.bfloat16),
@@ -505,23 +556,25 @@
         + [pl.BlockSpec(memory_space=pl.ANY)],
         out_specs=[pl.BlockSpec(memory_space=pltpu.VMEM)] * 2,
         scratch_shapes=[
-            pltpu.VMEM((2, count * rows, depth), jnp.bfloat16),
+            pltpu.VMEM((2, groups, count * GROUP, depth), jnp.bfloat16),
             pltpu.VMEM((diags * span,) + square, jnp.bfloat16),
             pltpu.VMEM((diags * span,) + square, jnp.bfloat16),
             pltpu.VMEM((2, keeps * span) + square, jnp.bfloat16),
-            pltpu.VMEM((products,) + (2,) * bits + block, jnp.bfloat16),
-            pltpu.VMEM((keeps,) + (2,) * (bits - 1) + block, jnp.bfloat16),
-            pltpu.VMEM((products,) + (2,) * (bits - 1) + block, jnp.bfloat16),
+            pltpu.VMEM((groups * products,) + (2,) * bits + block, jnp.bfloat16),
+            pltpu.VMEM((groups * keeps,) + (2,) * (bits - 1) + block, jnp.bfloat16),
+            pltpu.VMEM((groups * products,) + (2,) * (bits - 1) + block, jnp.bfloat16),
             *[
-                pltpu.VMEM((finals,) + (2,) * (bits - 1 - s) + block, jnp.bfloat16)
+                pltpu.VMEM((groups * finals,) + (2,) * (bits - 1 - s) + block, jnp.bfloat16)
                 for s in range(1, bits)
             ],
-            pltpu.VMEM((keeps,) + block, jnp.bfloat16),
-            pltpu.VMEM((keeps,) + block, jnp.bfloat16),
-            dma((4,)), dma,
-            dma((count,)), dma((count,)), dma((count,)), dma((count,)),
-            dma((products,)), dma((products,)), dma((keeps,)), dma((keeps,)),
-            dma((bits - 1, finals)), dma((bits - 1, finals)), dma((keeps,)), dma((keeps,)),
+            pltpu.VMEM((groups * keeps,) + block, jnp.bfloat16),
+            pltpu.VMEM((groups * keeps,) + block, jnp.bfloat16),
+            dma((4,)), dma((groups,)),
+            *[dma((groups, count))] * 4,
+            *[dma((groups * products,))] * 2,
+            *[dma((groups * keeps,))] * 2,
+            *[dma((bits - 1, groups * finals))] * 2,
+            *[dma((groups * keeps,))] * 2,
         ],
         compiler_params=pltpu.CompilerParams(
             collective_id=1, has_side_effects=True, vmem_limit_bytes=60 * 2**20
@@ -632,7 +685,9 @@
         and tile_width % (2 * STRIP) == 0
         and width == 2 * STRIP * STRIP
         and diag_cols == (strips + 1) * width
+        and rows_dev % GROUP == 0
         and lax.axis_size("cd") >= 2 * (strips + 1)
+        and lax.axis_size("cd") % 8 == 0
         and lax.axis_size("cd").bit_count() == 1
     )
     weights = ladder.reshape(out_rows // BLK, BLK, in_cols // BLK, BLK)
@@ -711,6 +766,8 @@
         tile_energy = (
             first_energy[None, :, None] + virt_energy.reshape(ab_count, 1, tile_width)
         ).reshape(1, cols_dev)
+        diag_rows = diag_rows.reshape(-1, rows_dev // GROUP, GROUP, 128)
+        diag_rows = jnp.swapaxes(diag_rows, 0, 1).reshape(rows_dev // GROUP, -1, 128)
         state = amplitudes.astype(jnp.bfloat16)
         for step in range(ITERS):
             sums, other = iteration_sums(state, diag_rows, masks, tiles_in, width)

time: 219 us -> 210 us (0.959)
  Pallas kernels: 204 us -> 195 us
    pallas_call x2, Pallas kernels: 193 us -> 183 us  [iteration_sums(): pl.pallas_call(functools.partial(iteration_kernel, bits, width, GROUP, gr...]
where the time goes in v5:
time: 210 us; the launch traced here: 209 us
  Pallas kernels  195 us (93%)
  local copies, waits for them, and re-layouts  9.67 us (5%)
  other arithmetic  4.62 us (2%)
    pallas_call x2, Pallas kernels, iteration_sums(): pl.pallas_call(functools.partial(iteration_kernel, bits, width, GROUP, gr...  183 us
    pallas_call x2, Pallas kernels, update(): pl.pallas_call(functools.partial(update_kernel, strips, STRIP, span), out...  11.4 us
    unnamed x14, local copies, waits for them, and re-layouts  5.06 us

profile of v5, /device:TPU:0, one launch (start us, length us, event | category | flops | bytes accessed | tf_op | source)
XLA Modules:
  0.0 209.2 jit_solution(2724326381464666979)
XLA Ops:
  0.0 0.7 dynamic_slice.6
  0.7 0.7 add.58
  1.5 0.8 compare_convert_fusion
  2.3 0.2 convolution_bitcast_fusion
  2.5 0.7 convert_element_type.17
  3.2 0.7 fusion.10
  3.9 0.1 copy.11
  4.0 0.1 broadcast_in_dim.25.rows_ref
  4.1 0.1 reshape.74
  4.2 0.1 broadcast_add_fusion
  4.3 0.1 add.61.cols_ref
  4.4 0.1 broadcast_in_dim.22
  4.6 0.9 broadcast_in_dim.20
  5.5 2.4 %convert_element_type.16.state_ref = bf16[48,8192]{1,0:T(8,128)(2,1)} convert(f32[48,8192]{1,0:T(8,128)} %param.7) | non-fusion elementwise | flops 393216 | bytes 2359296 | tf_op jit(solution)/shard_map/convert_element_type | solution.py:771
  7.9 1.6 broadcast_in_dim.24.mask_ref
  9.5 93.3 %shard_map.73 = (f32[48,4608]{1,0:T(8,128)}, bf16[48,2048]{1,0:T(8,128)(2,1)}) custom-call(bf16[48,8192]{1,0:T(8,128)(2,1)} %convert_element_type.16.state_ref, f32[3,256,128]{2,1,0:T(8,128)} %bitcast.14, bf16[2,32,16,1024]{3,2,1,0:T(8,128)(2,1)} %broadcast_in_dim.24.mask_ref, bf16[2,64,64,1024]{3,2,1,0:T(8,128)(2,1)} %bitcast.12), custom_call_target="tpu_custom_call" | custom-call | tf_op jit(solution)/shard_map/pallas_call | solution.py:549
  102.8 1.2 copy-done.4
  104.0 0.9 copy-done.6
  104.9 5.1 %shard_map.74.state_ref = bf16[48,8192]{1,0:T(8,128)(2,1)S(1)} custom-call(f32[48,4608]{1,0:T(8,128)S(1)} %copy-done.4, bf16[48,2048]{1,0:T(8,128)(2,1)S(1)} %copy-done.6, f32[48,8192]{1,0:T(8,128)S(1)} %copy-done.1, f32[1,8192]{1,0:T(1,128)S(1)} %add.61.cols_ref, f32[48,128]{1,0:T(8,128)S(1)} %broadcast_in_dim.25.rows_ref, ...), custom_call_target="tpu_custom_call" | custom-call | tf_op jit(solution)/shard_map/pallas_call | solution.py:661
  110.0 0.9 copy-done.2
  110.9 89.9 %shard_map.75 = (f32[48,4608]{1,0:T(8,128)}, bf16[48,2048]{1,0:T(8,128)(2,1)}) custom-call(bf16[48,8192]{1,0:T(8,128)(2,1)} %copy-done.2, f32[3,256,128]{2,1,0:T(8,128)} %bitcast.15, bf16[2,32,16,1024]{3,2,1,0:T(8,128)(2,1)} %broadcast_in_dim.24.mask_ref, bf16[2,64,64,1024]{3,2,1,0:T(8,128)(2,1)} %bitcast.13), custom_call_target="tpu_custom_call" | custom-call | tf_op jit(solution)/shard_map/pallas_call | solution.py:549
  200.9 1.2 copy-done.3
  202.0 0.9 copy-done.5
  202.9 6.3 %shard_map.76 = f32[48,8192]{1,0:T(8,128)} custom-call(f32[48,4608]{1,0:T(8,128)S(1)} %copy-done.3, bf16[48,2048]{1,0:T(8,128)(2,1)S(1)} %copy-done.5, f32[48,8192]{1,0:T(8,128)S(1)} %copy-done.1, f32[1,8192]{1,0:T(1,128)S(1)} %add.61.cols_ref, f32[48,128]{1,0:T(8,128)S(1)} %broadcast_in_dim.25.rows_ref, f32[48,128]{1,0:T(8,128)S(1)} %broadcast_in_dim.26.same_ref), custom_call_target="tpu_custom_call" | custom-call | tf_op jit(solution)/shard_map/pallas_call | solution.py:661
  (12 shorter events, 0.2 us)
Async XLA Ops:
  0.0 2.2 %copy-start = (f32[32]{0:T(128)S(1)}, f32[32]{0:T(128)}, u32[]{:S(2)}) copy-start(f32[32]{0:T(128)} %param.12) | copy-start | bytes 388
  9.5 93.3 %copy-start.1 = (f32[48,8192]{1,0:T(8,128)S(1)}, f32[48,8192]{1,0:T(8,128)}, u32[]{:S(2)}) copy-start(f32[48,8192]{1,0:T(8,128)} %driver_ref.3) | copy-start | bytes 4718596
  102.8 1.2 copy-start.4
  104.0 0.9 copy-start.6
  110.0 0.9 copy-start.2
  200.8 1.2 copy-start.3
  202.0 0.9 copy-start.5

commit v6 on v5

--- a/solution.py
+++ b/solution.py
@@ -170,7 +170,7 @@
 def iteration_kernel(
     bits, width, rows, groups,
     state_ref, diagonal_ref, mask_ref, weight_ref, sums_ref, other_ref,
-    low, straight, mirrored, outer, part, part_y, *rest,
+    state, low, straight, mirrored, outer, part, part_y, *rest,
 ):
     held = (part,) + rest[:bits]
     final, landed = rest[bits : bits + 2]
@@ -257,6 +257,7 @@
         outer[0, p] = masked(outer[0, p], 1 - ab, p // span).reshape(side, side, depth)
         outer[1, p] = turned(masked(outer[1, p], 1 - ab, kept_y(p, 1 - ab)))
 
+    state[...] = state_ref[...].astype(jnp.bfloat16)
     barrier = pltpu.get_barrier_semaphore()
 
     @pl.loop(1, count)
@@ -276,14 +277,14 @@
 
     def scatter(group, target, source):
         return remote(
-            state_ref.at[rows_of(group), cols_of(target)],
+            state.at[rows_of(group), cols_of(target)],
             low.at[0, group, rows_of(source), cols_of(ab)],
             a_send.at[group, target], a_recv.at[group, source], (ab, target),
         )
 
     def stay(group):
         return pltpu.make_async_copy(
-            state_ref.at[rows_of(group), cols_of(cd)],
+            state.at[rows_of(group), cols_of(cd)],
             low.at[0, group, rows_of(cd), cols_of(ab)],
             self_sem.at[group],
         )
@@ -406,8 +407,8 @@
     def dot(left, right):
         return lax.dot_general(left, right, NT, preferred_element_type=jnp.float32)
 
-    y_lag = 8
-    lags = [11 + 3 * stage for stage in range(bits - 1)]
+    y_lag = 7
+    lags = [10 + 3 * stage for stage in range(bits - 1)]
     sources = count // 8
 
     @pl.loop(0, (products * (groups * finals - 1)) // finals + lags[-1] + 1)
@@ -556,6 +557,7 @@
         + [pl.BlockSpec(memory_space=pl.ANY)],
         out_specs=[pl.BlockSpec(memory_space=pltpu.VMEM)] * 2,
         scratch_shapes=[
+            pltpu.VMEM(state.shape, jnp.bfloat16),
             pltpu.VMEM((2, groups, count * GROUP, depth), jnp.bfloat16),
             pltpu.VMEM((diags * span,) + square, jnp.bfloat16),
             pltpu.VMEM((diags * span,) + square, jnp.bfloat16),
@@ -577,7 +579,9 @@
             *[dma((groups * keeps,))] * 2,
         ],
         compiler_params=pltpu.CompilerParams(
-            collective_id=1, has_side_effects=True, vmem_limit_bytes=60 * 2**20
+            collective_id=1 if state.dtype == jnp.bfloat16 else 2,
+            has_side_effects=True,
+            vmem_limit_bytes=60 * 2**20,
         ),
     )(state, diagonal, mask, weights)
 
@@ -768,7 +772,7 @@
         ).reshape(1, cols_dev)
         diag_rows = diag_rows.reshape(-1, rows_dev // GROUP, GROUP, 128)
         diag_rows = jnp.swapaxes(diag_rows, 0, 1).reshape(rows_dev // GROUP, -1, 128)
-        state = amplitudes.astype(jnp.bfloat16)
+        state = amplitudes
         for step in range(ITERS):
             sums, other = iteration_sums(state, diag_rows, masks, tiles_in, width)
             state = update(

time: 210 us -> 206 us (0.981)
  other arithmetic: 4.62 us -> 2.26 us
    convert_element_type x1 -> x0, other arithmetic: 2.36 us -> none  [body(): state = amplitudes.astype(jnp.bfloat16)]
where the time goes in v6:
time: 206 us
  Pallas kernels  194 us (94%)
  local copies, waits for them, and re-layouts  9.67 us (5%)
  other arithmetic  2.26 us (1%)
    pallas_call x2, Pallas kernels, iteration_sums(): pl.pallas_call(functools.partial(iteration_kernel, bits, width, GROUP, gr...  182 us
    pallas_call x2, Pallas kernels, update(): pl.pallas_call(functools.partial(update_kernel, strips, STRIP, span), out...  11.4 us
    unnamed x14, local copies, waits for them, and re-layouts  5.06 us

profile of v6, /device:TPU:0, one launch (start us, length us, event | category | flops | bytes accessed | tf_op | source)
XLA Modules:
  0.0 205.8 jit_solution(1670129756748113648)
XLA Ops:
  0.0 0.7 dynamic_slice.6
  0.7 0.7 add.58
  1.5 0.8 compare_convert_fusion
  2.3 0.2 convolution_bitcast_fusion
  2.5 0.7 convert_element_type.13
  3.2 0.7 fusion.10
  3.9 0.1 copy.11
  4.0 0.1 broadcast_in_dim.25.rows_ref
  4.0 0.1 broadcast_in_dim.26.same_ref
  4.1 0.1 reshape.74
  4.2 0.1 broadcast_add_fusion
  4.3 0.1 add.61.cols_ref
  4.4 0.1 broadcast_in_dim.22
  4.6 0.9 broadcast_in_dim.20
  5.5 1.6 broadcast_in_dim.24.mask_ref
  7.1 92.9 %shard_map.73 = (f32[48,4608]{1,0:T(8,128)}, bf16[48,2048]{1,0:T(8,128)(2,1)}) custom-call(f32[48,8192]{1,0:T(8,128)} %state_ref.1, f32[3,256,128]{2,1,0:T(8,128)} %bitcast.14, bf16[2,32,16,1024]{3,2,1,0:T(8,128)(2,1)} %broadcast_in_dim.24.mask_ref, bf16[2,64,64,1024]{3,2,1,0:T(8,128)(2,1)} %bitcast.12), custom_call_target="tpu_custom_call" | custom-call | tf_op jit(solution)/shard_map/pallas_call | solution.py:550
  100.1 1.2 copy-done.4
  101.2 0.9 copy-done.6
  102.1 5.1 %shard_map.74.state_ref = bf16[48,8192]{1,0:T(8,128)(2,1)S(1)} custom-call(f32[48,4608]{1,0:T(8,128)S(1)} %copy-done.4, bf16[48,2048]{1,0:T(8,128)(2,1)S(1)} %copy-done.6, f32[48,8192]{1,0:T(8,128)S(1)} %copy-done.1, f32[1,8192]{1,0:T(1,128)S(1)} %add.61.cols_ref, f32[48,128]{1,0:T(8,128)S(1)} %broadcast_in_dim.25.rows_ref, ...), custom_call_target="tpu_custom_call" | custom-call | tf_op jit(solution)/shard_map/pallas_call | solution.py:665
  107.3 0.9 copy-done.2
  108.2 89.3 %shard_map.75 = (f32[48,4608]{1,0:T(8,128)}, bf16[48,2048]{1,0:T(8,128)(2,1)}) custom-call(bf16[48,8192]{1,0:T(8,128)(2,1)} %copy-done.2, f32[3,256,128]{2,1,0:T(8,128)} %bitcast.15, bf16[2,32,16,1024]{3,2,1,0:T(8,128)(2,1)} %broadcast_in_dim.24.mask_ref, bf16[2,64,64,1024]{3,2,1,0:T(8,128)(2,1)} %bitcast.13), custom_call_target="tpu_custom_call" | custom-call | tf_op jit(solution)/shard_map/pallas_call | solution.py:550
  197.5 1.2 copy-done.3
  198.6 0.9 copy-done.5
  199.5 6.3 %shard_map.76 = f32[48,8192]{1,0:T(8,128)} custom-call(f32[48,4608]{1,0:T(8,128)S(1)} %copy-done.3, bf16[48,2048]{1,0:T(8,128)(2,1)S(1)} %copy-done.5, f32[48,8192]{1,0:T(8,128)S(1)} %copy-done.1, f32[1,8192]{1,0:T(1,128)S(1)} %add.61.cols_ref, f32[48,128]{1,0:T(8,128)S(1)} %broadcast_in_dim.25.rows_ref, f32[48,128]{1,0:T(8,128)S(1)} %broadcast_in_dim.26.same_ref), custom_call_target="tpu_custom_call" | custom-call | tf_op jit(solution)/shard_map/pallas_call | solution.py:665
  (11 shorter events, 0.1 us)
Async XLA Ops:
  0.0 2.2 %copy-start = (f32[32]{0:T(128)S(1)}, f32[32]{0:T(128)}, u32[]{:S(2)}) copy-start(f32[32]{0:T(128)} %param.12) | copy-start | bytes 388
  7.1 92.9 %copy-start.1 = (f32[48,8192]{1,0:T(8,128)S(1)}, f32[48,8192]{1,0:T(8,128)}, u32[]{:S(2)}) copy-start(f32[48,8192]{1,0:T(8,128)} %driver_ref.3) | copy-start | bytes 4718596
  100.0 1.2 copy-start.4
  101.2 0.9 copy-start.6
  107.3 0.9 copy-start.2
  197.4 1.2 copy-start.3
  198.6 0.9 copy-start.5

commit v7 on v6

--- a/solution.py
+++ b/solution.py
@@ -336,6 +336,11 @@
     def _(i):
         pass_on(0, i)
 
+        if groups > 1:
+            @pl.when(i == count - 4)
+            def _():
+                send_group(1)
+
         @pl.when(i == 0)
         def _():
             pltpu.make_async_copy(straight, straight, load_sem.at[0]).wait()
@@ -355,9 +360,6 @@
         @pl.when(late >= 0)
         def _():
             prepare_outer(late)
-
-    if groups > 1:
-        send_group(1)
 
     @pl.loop(0, count)
     def _(i):

time: 206 us -> 207 us (level)
  no operation moved by 1% of the time
where the time goes in v7:
time: 207 us
  Pallas kernels  195 us (94%)
  local copies, waits for them, and re-layouts  9.67 us (5%)
  other arithmetic  2.26 us (1%)
    pallas_call x2, Pallas kernels, iteration_sums(): pl.pallas_call(functools.partial(iteration_kernel, bits, width, GROUP, gr...  183 us
    pallas_call x2, Pallas kernels, update(): pl.pallas_call(functools.partial(update_kernel, strips, STRIP, span), out...  11.4 us
    unnamed x14, local copies, waits for them, and re-layouts  5.06 us

profile of v7, /device:TPU:0, one launch (start us, length us, event | category | flops | bytes accessed | tf_op | source)
XLA Modules:
  0.0 207.1 jit_solution(321299649169277137)
XLA Ops:
  0.0 0.7 dynamic_slice.6
  0.7 0.7 add.58
  1.5 0.8 compare_convert_fusion
  2.3 0.2 convolution_bitcast_fusion
  2.5 0.7 convert_element_type.13
  3.2 0.7 fusion.10
  3.9 0.1 copy.11
  4.0 0.1 broadcast_in_dim.25.rows_ref
  4.0 0.1 broadcast_in_dim.26.same_ref
  4.1 0.1 reshape.74
  4.2 0.1 broadcast_add_fusion
  4.3 0.1 add.61.cols_ref
  4.4 0.1 broadcast_in_dim.22
  4.6 0.9 broadcast_in_dim.20
  5.5 1.6 broadcast_in_dim.24.mask_ref
  7.1 93.5 %shard_map.73 = (f32[48,4608]{1,0:T(8,128)}, bf16[48,2048]{1,0:T(8,128)(2,1)}) custom-call(f32[48,8192]{1,0:T(8,128)} %state_ref.1, f32[3,256,128]{2,1,0:T(8,128)} %bitcast.14, bf16[2,32,16,1024]{3,2,1,0:T(8,128)(2,1)} %broadcast_in_dim.24.mask_ref, bf16[2,64,64,1024]{3,2,1,0:T(8,128)(2,1)} %bitcast.12), custom_call_target="tpu_custom_call" | custom-call | tf_op jit(solution)/shard_map/pallas_call | solution.py:552
  100.7 1.2 copy-done.4
  101.8 0.9 copy-done.6
  102.7 5.1 %shard_map.74.state_ref = bf16[48,8192]{1,0:T(8,128)(2,1)S(1)} custom-call(f32[48,4608]{1,0:T(8,128)S(1)} %copy-done.4, bf16[48,2048]{1,0:T(8,128)(2,1)S(1)} %copy-done.6, f32[48,8192]{1,0:T(8,128)S(1)} %copy-done.1, f32[1,8192]{1,0:T(1,128)S(1)} %add.61.cols_ref, f32[48,128]{1,0:T(8,128)S(1)} %broadcast_in_dim.25.rows_ref, ...), custom_call_target="tpu_custom_call" | custom-call | tf_op jit(solution)/shard_map/pallas_call | solution.py:667
  107.9 0.9 copy-done.2
  108.8 90.0 %shard_map.75 = (f32[48,4608]{1,0:T(8,128)}, bf16[48,2048]{1,0:T(8,128)(2,1)}) custom-call(bf16[48,8192]{1,0:T(8,128)(2,1)} %copy-done.2, f32[3,256,128]{2,1,0:T(8,128)} %bitcast.15, bf16[2,32,16,1024]{3,2,1,0:T(8,128)(2,1)} %broadcast_in_dim.24.mask_ref, bf16[2,64,64,1024]{3,2,1,0:T(8,128)(2,1)} %bitcast.13), custom_call_target="tpu_custom_call" | custom-call | tf_op jit(solution)/shard_map/pallas_call | solution.py:552
  198.7 1.2 copy-done.3
  199.9 0.9 copy-done.5
  200.8 6.3 %shard_map.76 = f32[48,8192]{1,0:T(8,128)} custom-call(f32[48,4608]{1,0:T(8,128)S(1)} %copy-done.3, bf16[48,2048]{1,0:T(8,128)(2,1)S(1)} %copy-done.5, f32[48,8192]{1,0:T(8,128)S(1)} %copy-done.1, f32[1,8192]{1,0:T(1,128)S(1)} %add.61.cols_ref, f32[48,128]{1,0:T(8,128)S(1)} %broadcast_in_dim.25.rows_ref, f32[48,128]{1,0:T(8,128)S(1)} %broadcast_in_dim.26.same_ref), custom_call_target="tpu_custom_call" | custom-call | tf_op jit(solution)/shard_map/pallas_call | solution.py:667
  (11 shorter events, 0.1 us)
Async XLA Ops:
  0.0 2.2 %copy-start = (f32[32]{0:T(128)S(1)}, f32[32]{0:T(128)}, u32[]{:S(2)}) copy-start(f32[32]{0:T(128)} %param.12) | copy-start | bytes 388
  7.1 93.5 %copy-start.1 = (f32[48,8192]{1,0:T(8,128)S(1)}, f32[48,8192]{1,0:T(8,128)}, u32[]{:S(2)}) copy-start(f32[48,8192]{1,0:T(8,128)} %driver_ref.3) | copy-start | bytes 4718596
  100.6 1.2 copy-start.4
  101.8 0.9 copy-start.6
  107.9 0.9 copy-start.2
  198.7 1.2 copy-start.3
  199.9 0.9 copy-start.5
